TPU v7x, 32 devices: a whole 2x2x4 slice. The times are simulated.
32 devices in a mesh: pw: 8 (over z, core), band: 4 (over y, x).
Axes of the slice: x: 2, y: 2, z: 4, core: 2. Of those that a mesh axis runs over, the one named last changes fastest.
Arguments:
- psi_res: bfloat16 [256, 2, 72, 1024], P('band', None, None, 'pw'), may hold values from -0.015625 to 0.015625
- correction: float32 [4, 2, 72, 1024], P('band', None, None, 'pw'), may hold values from -24 to 24
- local_potential: float32 [128, 128, 128], P('pw'), may hold values from -2 to 1
- stick_xy: int32 [1024], P('pw'), may hold values from 0 to 16383, as said below
Outputs:
- residual: float32 [4, 2, 72, 1024], P('band', None, None, 'pw')
- hamiltonian_proj: float32 [2, 256, 4], P(None, 'band')
- intersection_proj: float32 [2, 256, 4], P(None, 'band')
Inputs may be any that keep to these rules, and one draw needn't show every extreme that they name: `stick_xy`: distinct positions: the 1024 positions of the x-y plane nearest the anchor of the periodic grid, ties broken at random, in an order drawn from the seed.
All inputs are finite; a program needn't handle non-finite values.
Results may differ from a plain program's by a relative error of at most 0.0029.
Values may be sent and summed in bfloat16 or wider, within the bound.
No kernel may reach another device: no remote copies, remote signals or barrier semaphores. Data moves between devices by JAX's collectives and lax.ppermute only.
A program may use at most 128 MiB of HBM per device.

v0:
```python
import math

import jax
import jax.numpy as jnp
import numpy as np
from jax import lax
from jax.experimental import pallas as pl
from jax.experimental.pallas import tpu as pltpu
from jax.sharding import PartitionSpec as P

kinetic_unit = 0.002
highest = lax.Precision.HIGHEST
lanes = 128
f32 = jnp.float32
bf16 = jnp.bfloat16


def round_up(count, step):
    return -(-count // step) * step


def signed_freq(index, grid_size):
    return jnp.where(index < grid_size // 2, index, index - grid_size)


def phases(out_index, in_index, direction, grid_size):
    angles = (out_index[:, None] * in_index[None, :]) % grid_size * (2.0 * math.pi / grid_size)
    cosine, sine = np.cos(angles), direction * np.sin(angles)
    return np.stack([np.stack([cosine, -sine], 1), np.stack([sine, cosine], 1)], 0)


def split(table, count):
    pieces = []
    rest = np.asarray(table, np.float64)
    for _ in range(count):
        piece = rest.astype(jnp.bfloat16)
        pieces.append(piece)
        rest = rest - piece.astype(np.float64)
    return pieces


class Sizes:
    def __init__(self, groups, planes, grid_size, stick_depth, sticks_local):
        self.groups, self.planes = groups, planes
        self.grid, self.depth, self.sticks_local = grid_size, stick_depth, sticks_local
        self.rows = round_up(planes, 16)
        self.sticks = groups * sticks_local
        self.box = round_up(2 * math.ceil(math.sqrt(self.sticks / math.pi)) + 2, 8)
        self.pair = 2 * self.box
        self.pair_pad = round_up(self.pair, lanes)


def z_rows(sizes):
    group = np.repeat(np.arange(sizes.groups), sizes.rows)
    plane = np.tile(np.arange(sizes.rows), sizes.groups)
    return group * sizes.planes + plane, plane < sizes.planes


def z_back_table(sizes):
    z_freq = np.arange(sizes.depth) - sizes.depth // 2
    z_index, real = z_rows(sizes)
    table = phases(z_index, z_freq, 1, sizes.grid) * real[None, :, None, None]
    table = table.reshape(2, sizes.groups, sizes.rows, 2 * sizes.depth)
    return table.transpose(1, 0, 2, 3).reshape(-1, 2 * sizes.depth).astype(np.float32)


def z_forward_table(sizes):
    z_freq = np.arange(sizes.depth) - sizes.depth // 2
    z_index, real = z_rows(sizes)
    table = phases(z_freq, z_index, -1, sizes.grid) * real / float(sizes.grid**3)
    table = table.reshape(2 * sizes.depth, 2, sizes.groups, sizes.rows)
    table = table.transpose(0, 2, 1, 3).reshape(2 * sizes.depth, -1)
    return np.concatenate(split(table, 3), 0)


def plane_tables(sizes):
    grid = np.arange(sizes.grid)
    freq = np.arange(sizes.box) - sizes.box // 2
    back = phases(grid, freq, 1, sizes.grid).reshape(2 * sizes.grid, sizes.pair)
    forward = phases(freq, grid, -1, sizes.grid).reshape(sizes.pair, 2 * sizes.grid)
    back_high, back_low = split(back, 2)
    forward_high, forward_low = split(forward, 2)
    pad = ((0, sizes.pair_pad - sizes.pair), (0, 0))
    y_back = np.concatenate([np.pad(back_high.T, pad), np.pad(back_low.T, pad)], 0)
    x_back = np.concatenate([back_high, back_low, back_high], 1)
    x_forward = np.concatenate([forward_high, forward_low], 0)
    y_forward = np.concatenate([np.pad(forward_high, pad), np.pad(forward_low, pad)], 0).T
    return y_back, x_back, x_forward, y_forward


def vmem():
    return pl.BlockSpec(memory_space=pltpu.VMEM)


def spread_sticks(sizes, vector, positions):
    def kernel(table_ref, vector_ref, position_ref, out_ref):
        columns = jnp.dot(table_ref[...], vector_ref[...], precision=highest, preferred_element_type=f32)
        block = 2 * sizes.rows
        x_pos = (position_ref[...] // sizes.grid).astype(f32)
        y_pos = (position_ref[...] % sizes.grid).astype(f32)
        row = lax.broadcasted_iota(jnp.int32, (16, sizes.sticks_local), 0)
        tail = jnp.where(row == 0, x_pos, jnp.where(row == 1, y_pos, 0.0)).astype(bf16)
        for group in range(sizes.groups):
            out_ref[group, 0:block, :] = columns[group * block : (group + 1) * block].astype(bf16)
            out_ref[group, block:, :] = tail

    return pl.pallas_call(
        kernel,
        out_shape=jax.ShapeDtypeStruct((sizes.groups, 2 * sizes.rows + 16, sizes.sticks_local), bf16),
        in_specs=[vmem()] * 3,
        out_specs=vmem(),
        name="spread_sticks",
    )(jnp.asarray(z_back_table(sizes)), vector, positions[None, :])


def anchor_of(position, grid_size):
    angle = position * (2.0 * math.pi / grid_size)
    spot = lax.broadcasted_iota(jnp.int32, (1, grid_size), 1).astype(f32)
    spot_angle = spot * (2.0 * math.pi / grid_size)

    def total(values):
        return jnp.sum(jnp.sum(values, axis=0, keepdims=True), axis=1, keepdims=True)

    score = total(jnp.cos(angle)) * jnp.cos(spot_angle) + total(jnp.sin(angle)) * jnp.sin(spot_angle)
    best = jnp.max(score, axis=1, keepdims=True)
    return jnp.min(jnp.where(score >= best, spot, float(grid_size)), axis=1, keepdims=True)


def apply_planes(sizes, received, potential):
    grid, box, pair, pair_pad, rows = sizes.grid, sizes.box, sizes.pair, sizes.pair_pad, sizes.rows
    groups, local, sticks = sizes.groups, sizes.sticks_local, sizes.sticks
    y_back, x_back, x_forward, y_forward = plane_tables(sizes)

    def kernel(in_ref, pot_ref, yb_ref, xb_ref, xf_ref, yf_ref, out_ref, left_ref, hot_ref, a_ref, b_ref):
        def relative(position):
            moved = position - anchor_of(position, grid) + float(box // 2)
            moved = jnp.where(moved < 0, moved + float(grid), moved)
            return jnp.where(moved >= float(grid), moved - float(grid), moved)

        x_rel = relative(jnp.concatenate([in_ref[g, 2 * rows : 2 * rows + 16, :].astype(f32)[0:1] for g in range(groups)], 0))
        y_rel = relative(jnp.concatenate([in_ref[g, 2 * rows : 2 * rows + 16, :].astype(f32)[1:2] for g in range(groups)], 0))

        y_row = lax.broadcasted_iota(jnp.int32, (pair_pad, local), 0).astype(f32)
        for g in range(groups):
            y_here = jnp.broadcast_to(y_rel[g : g + 1], (pair_pad, local))
            for part in range(2):
                hot = jnp.where(y_row == y_here + float(part * box), 1.0, 0.0)
                hot = jnp.where(y_row < float((part + 1) * box), hot, 0.0).astype(bf16)
                where = part * sticks + g * local
                hot_ref[0:pair_pad, where : where + local] = hot
                hot_ref[pair_pad:, where : where + local] = hot
            x_here = jnp.broadcast_to(x_rel[g : g + 1], (rows, local))
            parts = [in_ref[g, part * rows : (part + 1) * rows, :].astype(f32) for part in range(2)]
            for x in range(box):
                mask = x_here == float(x)
                for part in range(2):
                    where = part * sticks + g * local
                    left_ref[x * rows : (x + 1) * rows, where : where + local] = jnp.where(mask, parts[part], 0.0).astype(bf16)

        placed = lax.dot_general(left_ref[...], hot_ref[...], (((1,), (1,)), ((), ())), preferred_element_type=f32)
        lines = jnp.dot(placed.astype(bf16), yb_ref[...], preferred_element_type=f32)
        for part in range(2):
            a_ref[part] = lines[:, part * grid : (part + 1) * grid]

        for first in range(0, rows, 2):
            both = range(first, first + 2)
            high, low = [], []
            for plane in both:
                lines = jnp.concatenate([a_ref[part, pl.ds(plane, box, stride=rows), :] for part in range(2)], 0)
                high.append(lines.astype(bf16))
                low.append((lines - high[-1].astype(f32)).astype(bf16))
            high, low = jnp.concatenate(high, 1), jnp.concatenate(low, 1)
            field = jnp.dot(xb_ref[...], jnp.concatenate([high, high, low], 0), preferred_element_type=f32)
            weight = jnp.concatenate([pot_ref[plane] for plane in both], 1)
            field = (field * jnp.concatenate([weight, weight], 0)).astype(bf16)
            back = jnp.dot(xf_ref[...], field, preferred_element_type=f32)
            back = back[:pair] + back[pair:]
            for index, plane in enumerate(both):
                mine = back[:, index * grid : (index + 1) * grid]
                for part in range(2):
                    b_ref[part, pl.ds(plane, box, stride=rows), :] = mine[part * box : (part + 1) * box]

        lines = jnp.concatenate([b_ref[0], b_ref[1]], 1)
        high = lines.astype(bf16)
        low = (lines - high.astype(f32)).astype(bf16)
        boxed = jnp.dot(high, yf_ref[...], preferred_element_type=f32)
        boxed = boxed[:, :pair_pad] + boxed[:, pair_pad:]
        boxed = boxed + jnp.dot(low, yf_ref[:, :pair_pad], preferred_element_type=f32)
        boxed = boxed.astype(bf16)
        for part in range(2):
            for g in range(groups):
                where = part * sticks + g * local
                found = jnp.dot(boxed, hot_ref[0:pair_pad, where : where + local], preferred_element_type=f32)
                x_here = jnp.broadcast_to(x_rel[g : g + 1], (rows, local))
                total = jnp.zeros((rows, local), f32)
                for x in range(box):
                    total = total + jnp.where(x_here == float(x), found[x * rows : (x + 1) * rows], 0.0)
                out_ref[g, part * rows : (part + 1) * rows, :] = total.astype(bf16)

    return pl.pallas_call(
        kernel,
        out_shape=jax.ShapeDtypeStruct((groups, 2 * rows, local), bf16),
        in_specs=[vmem()] * 6,
        out_specs=vmem(),
        scratch_shapes=[
            pltpu.VMEM((box * rows, 2 * sticks), bf16),
            pltpu.VMEM((2 * pair_pad, 2 * sticks), bf16),
            pltpu.VMEM((2, box * rows, grid), f32),
            pltpu.VMEM((2, box * rows, grid), f32),
        ],
        name="apply_planes",
    )(received, potential, *[jnp.asarray(t) for t in (y_back, x_back, x_forward, y_forward)])


def image_sticks(sizes, columns, vector, positions):
    depth, local, grid = sizes.depth, sizes.sticks_local, sizes.grid
    height = 2 * depth

    def kernel(table_ref, columns_ref, vector_ref, position_ref, image_ref, rounded_ref, sums_ref):
        product = jnp.dot(table_ref[...], columns_ref[...], preferred_element_type=f32)
        applied = product[:height] + (product[height : 2 * height] + product[2 * height :])
        vector = vector_ref[...]
        x_freq = signed_freq(position_ref[...] // grid, grid)
        y_freq = signed_freq(position_ref[...] % grid, grid)
        row = lax.broadcasted_iota(jnp.int32, (height, local), 0)
        z_freq = jnp.where(row < depth, row, row - depth) - depth // 2
        kinetic = kinetic_unit * (z_freq * z_freq + (x_freq * x_freq + y_freq * y_freq)).astype(f32)
        image = kinetic * vector + applied
        image_ref[...] = image
        rounded_ref[0:height, :] = vector.astype(bf16)
        rounded_ref[height:, :] = image.astype(bf16)
        sums_ref[0:1, :] = jnp.sum(vector * image, axis=0, keepdims=True)
        sums_ref[1:2, :] = jnp.sum(vector * vector, axis=0, keepdims=True)

    return pl.pallas_call(
        kernel,
        out_shape=(
            jax.ShapeDtypeStruct((height, local), f32),
            jax.ShapeDtypeStruct((2 * height, local), bf16),
            jax.ShapeDtypeStruct((2, local), f32),
        ),
        in_specs=[vmem()] * 4,
        out_specs=(vmem(),) * 3,
        name="image_sticks",
    )(jnp.asarray(z_forward_table(sizes)), columns, vector, positions[None, :])


def shards(psi_res, correction, local_potential, stick_xy):
    groups = lax.axis_size("pw")
    planes, grid_size = local_potential.shape[:2]
    band_count, _, stick_depth, sticks_local = correction.shape
    res_count = psi_res.shape[0]
    sizes = Sizes(groups, planes, grid_size, stick_depth, sticks_local)
    length = stick_depth * sticks_local
    potential = jnp.pad(local_potential, ((0, sizes.rows - planes), (0, 0), (0, 0)))

    images, rounded, sums = [], [], []
    for band in range(band_count):
        vector = correction[band].reshape(2 * stick_depth, sticks_local)
        moving = spread_sticks(sizes, vector, stick_xy)
        moving = lax.all_to_all(moving, "pw", split_axis=0, concat_axis=0, tiled=True)
        picked = apply_planes(sizes, moving, potential)
        picked = lax.all_to_all(picked, "pw", split_axis=0, concat_axis=0, tiled=True)
        picked = picked.reshape(2 * sizes.rows * groups, sticks_local)
        one_image, one_rounded, one_sums = image_sticks(sizes, picked, vector, stick_xy)
        images.append(one_image)
        rounded.append(one_rounded)
        sums.append(one_sums)
    image = jnp.stack(images, 0).reshape(correction.shape)
    rounded = jnp.stack(rounded, 0)

    rows = lax.all_gather(rounded, "band", axis=0, tiled=True)
    row_count = rows.shape[0]
    rows = rows.reshape(row_count, 2, 2, length)
    straight = jnp.transpose(rows, (1, 0, 2, 3))
    turned = jnp.stack([straight[:, :, 1], -straight[:, :, 0]], 2)
    joined = jnp.stack([straight, turned], 1).reshape(4 * row_count, 2 * length)
    product = lax.dot_general(
        joined, psi_res.reshape(res_count, 2 * length), (((1,), (1,)), ((), ())), preferred_element_type=f32
    )
    flat = product.reshape(-1)
    tail = jnp.concatenate(sums, 0).reshape(-1)
    total_length = flat.shape[0] + tail.shape[0]
    padded = round_up(total_length, 8 * lanes)
    flat = jnp.concatenate([flat, tail, jnp.zeros((padded - total_length,), f32)]).reshape(-1, lanes)
    copies = jnp.broadcast_to(flat[None], (groups,) + flat.shape)
    copies = lax.all_to_all(copies, "pw", split_axis=0, concat_axis=0, tiled=True)
    total = jnp.sum(copies, axis=0).reshape(-1)
    product = total[: product.size].reshape(2, 2, row_count, res_count)
    product = jnp.transpose(product, (0, 1, 3, 2))
    tail = total[product.size : total_length].reshape(band_count, 2, sticks_local)
    tail = jnp.sum(tail, axis=2)
    rayleigh = tail[:, 0] / tail[:, 1]
    residual = image - rayleigh[:, None, None, None] * correction
    return (residual, product[1], product[0])


def solution(mesh):
    return jax.shard_map(
        shards,
        mesh=mesh,
        in_specs=(
            P("band", None, None, "pw"),
            P("band", None, None, "pw"),
            P("pw", None, None),
            P("pw"),
        ),
        out_specs=(P("band", None, None, "pw"), P(None, "band", None), P(None, "band", None)),
        check_vma=False,
    )
```

profile of v0, /device:TPU:0, one launch (start us, length us, event | category | flops | bytes accessed | tf_op | source)
XLA Modules:
  0.0 58.8 jit_solution(10726476844556263335)
XLA Ops:
  0.6 2.0 %spread_sticks.1 = bf16[8,48,128]{2,1,0:T(8,128)(2,1)} custom-call(f32[256,144]{1,0:T(8,128)} %constant.8.clone.table_ref, f32[144,128]{1,0:T(8,128)} %bitcast.38, s32[1,128]{1,0:T(1,128)} %bitcast.43), custom_call_target="tpu_custom_call" | custom-call | tf_op jit(solution)/shard_map/spread_sticks/pallas_call | solution.py:107
  2.6 12.8 %all_to_all.15.in_ref = bf16[8,48,128]{2,1,0:T(8,128)(2,1)} all-to-all(bf16[8,48,128]{2,1,0:T(8,128)(2,1)} %spread_sticks.1), channel_id=1, replica_groups=mesh['pw'=8,'band'=4] {'pw'}, dimensions={0} | all-to-all | bytes 196608 | tf_op jit(solution)/shard_map/all_to_all | solution.py:261
  15.4 7.2 %apply_planes.1 = bf16[8,32,128]{2,1,0:T(8,128)(2,1)} custom-call(bf16[8,48,128]{2,1,0:T(8,128)(2,1)} %all_to_all.15.in_ref, f32[16,128,128]{2,1,0:T(8,128)} %pot_ref.1, bf16[256,256]{1,0:T(8,128)(2,1)} %constant.6.clone.yb_ref, bf16[256,240]{1,0:T(8,128)(2,1)} %constant.18.clone.xb_ref, bf16[160,256]{1,0:T(8,128)(2,1)} %constant.19.clone.xf_ref, ...), custom_call_target="tpu_custom_call" | custom-call | tf_op jit(solution)/shard_map/apply_planes/pallas_call | solution.py:200
  22.6 9.9 %all_to_all.16 = bf16[8,32,128]{2,1,0:T(8,128)(2,1)} all-to-all(bf16[8,32,128]{2,1,0:T(8,128)(2,1)} %apply_planes.1), channel_id=1, replica_groups=mesh['pw'=8,'band'=4] {'pw'}, dimensions={0} | all-to-all | bytes 131072 | tf_op jit(solution)/shard_map/all_to_all | solution.py:263
  32.4 1.9 %image_sticks.1 = (f32[144,128]{1,0:T(8,128)}, bf16[288,128]{1,0:T(8,128)(2,1)}, f32[2,128]{1,0:T(2,128)}) custom-call(bf16[432,256]{1,0:T(8,128)(2,1)} %constant.21.clone.table_ref, bf16[256,128]{1,0:T(8,128)(2,1)} %bitcast.40, f32[144,128]{1,0:T(8,128)} %bitcast.39, s32[1,128]{1,0:T(1,128)} %bitcast.44), custom_call_target="tpu_custom_call" | custom-call | tf_op jit(solution)/shard_map/image_sticks/pallas_call | solution.py:235
  34.3 9.4 %all-gather = bf16[1152,128]{1,0:T(8,128)(2,1)S(1)} all-gather(bf16[288,128]{1,0:T(8,128)(2,1)} %get-tuple-element.7), channel_id=2, replica_groups=mesh['pw'=8,'band'=4] {'band'}, dimensions={0}, use_global_device_ids=true | all-gather | bytes 368640 | tf_op jit(solution)/shard_map/all_gather | solution.py:272
  43.8 0.1 reshape.41
  43.8 0.2 copy.25
  44.1 0.0 copy-start
  44.1 0.5 fusion.3
  44.6 0.7 %maximum_bitcast_fusion = bf16[2,1,4,2,9216]{4,3,2,1,0:T(2,128)(2,1)S(1)} fusion(bf16[2,4,1,9216]{3,2,1,0:T(2,128)(2,1)S(1)} %get-tuple-element.12, bf16[2,4,1,9216]{3,2,1,0:T(2,128)(2,1)S(1)} %get-tuple-element.11), kind=kLoop, calls=%fused_computation.5 | loop fusion | flops 589824 | bytes 589824 | tf_op jit(solution)/shard_map/stack | solution.py:277
  45.3 0.8 %pad_maximum_fusion = bf16[2,2,4,2,9216]{4,3,2,1,0:T(2,128)(2,1)S(1)} fusion(bf16[2,1,4,2,9216]{4,3,2,1,0:T(2,128)(2,1)S(1)} %maximum_bitcast_fusion, bf16[2,1,4,2,9216]{4,3,2,1,0:T(2,128)(2,1)S(1)} %bitcast.34), kind=kLoop, calls=%fused_computation.3 | loop fusion | flops 294912 | bytes 1179648 | tf_op jit(solution)/shard_map/stack | solution.py:277
  46.1 0.0 copy-start.3
  46.1 0.0 copy-start.1
  46.1 0.0 copy-start.2
  46.2 0.1 copy.17
  46.3 0.0 copy-done
  46.3 0.7 %fusion = f32[16,64]{1,0:T(8,128)S(1)} fusion(bf16[16,18432]{1,0:T(8,128)(2,1)S(1)} %bitcast.37, bf16[8,8,144,128]{3,2,1,0:T(8,128)(2,1)S(1)} %bitcast.35), kind=kOutput, calls=%fused_computation | convolution fusion | flops 37748736 | bytes 2953216 | tf_op jit(solution)/shard_map/dot_general | solution.py:278
  47.0 0.1 reshape.44
  47.1 0.0 copy-done.3
  47.1 8.3 %all_to_all.17 = f32[8,16,128]{2,1,0:T(8,128)S(1)} all-to-all(f32[8,16,128]{2,1,0:T(8,128)S(1)} %broadcast_in_dim.18), channel_id=1, replica_groups=mesh['pw'=8,'band'=4] {'pw'}, dimensions={0} | all-to-all | bytes 131072 | tf_op jit(solution)/shard_map/all_to_all | solution.py:287
  55.4 0.1 slice_reduce_fusion
  55.5 0.6 %fusion.4 = (f32[1,1]{1,0:T(1,128)}, f32[1,1]{1,0:T(1,128)}) fusion(f32[1,2]{1,0:T(1,128)S(1)} %bitcast.45), kind=kLoop, calls=%fused_computation.14 | loop fusion | bytes 16 | tf_op jit(solution)/shard_map/slice | solution.py:293
  56.2 0.1 reshape.46
  56.3 0.6 %slice_bitcast_fusion = (f32[2,64,4]{1,2,0:T(4,128)}, f32[2,64,4]{1,2,0:T(4,128)}) fusion(f32[2,2,64,4]{2,3,1,0:T(4,128)S(1)} %bitcast.42), kind=kLoop, calls=%fused_computation.10 | loop fusion | bytes 8192 | tf_op jit(solution)/shard_map/squeeze | solution.py:295
  58.1 0.0 copy-done.1
  58.2 0.0 copy-done.2
  58.2 0.6 %multiply_subtract_fusion = f32[1,2,72,128]{3,2,1,0:T(8,128)} fusion(f32[1,2,72,128]{3,2,1,0:T(8,128)S(1)} %bitcast.41, f32[1,2,72,128]{3,2,1,0:T(8,128)S(1)} %copy-done.1, f32[]{:T(128)} %bitcast.11), kind=kLoop, calls=%fused_computation.8 | loop fusion | flops 36864 | bytes 221188 | tf_op jit(solution)/shard_map/sub | solution.py:294
  (5 shorter events, 0.0 us)
Async XLA Ops:
  44.1 2.2 %copy-start = (bf16[64,2,72,128]{3,2,1,0:T(8,128)(2,1)S(1)}, bf16[64,2,72,128]{3,2,1,0:T(8,128)(2,1)}, u32[]{:S(2)}) copy-start(bf16[64,2,72,128]{3,2,1,0:T(8,128)(2,1)} %param.10) | copy-start | bytes 7077892
  46.1 0.9 %copy-start.3 = (f32[2,128]{1,0:T(2,128)S(1)}, f32[2,128]{1,0:T(2,128)}, u32[]{:S(2)}) copy-start(f32[2,128]{1,0:T(2,128)} %get-tuple-element.8) | copy-start | bytes 3076
  46.1 12.0 %copy-start.1 = (f32[1,2,72,128]{3,2,1,0:T(8,128)S(1)}, f32[1,2,72,128]{3,2,1,0:T(8,128)}, u32[]{:S(2)}) copy-start(f32[1,2,72,128]{3,2,1,0:T(8,128)} %param.11) | copy-start | bytes 221188
  46.1 12.0 %copy-start.2 = (f32[144,128]{1,0:T(8,128)S(1)}, f32[144,128]{1,0:T(8,128)}, u32[]{:S(2)}) copy-start(f32[144,128]{1,0:T(8,128)} %get-tuple-element.6) | copy-start | bytes 221188
where the time goes:
time: 59.3 us; the launch traced here: 58.8 us
  blocking collectives  40.4 us (68%)
  Pallas kernels  11.1 us (19%)
  other arithmetic  2.82 us (5%)
  between operations  2.04 us (3%)
  local copies, waits for them, and re-layouts  1.81 us (3%)
  matrix products  0.72 us (1%)
    all_to_all x1, blocking collectives, shards(): lax.all_to_all(moving, 'pw', split_axis=0, concat_axis=0, tiled=True)  12.8 us
    all_to_all x1, blocking collectives, shards(): lax.all_to_all(picked, 'pw', split_axis=0, concat_axis=0, tiled=True)  9.87 us
    all_gather x1, blocking collectives, shards(): rows = lax.all_gather(rounded, 'band', axis=0, tiled=True)  9.44 us
    all_to_all x1, blocking collectives, shards(): lax.all_to_all(copies, 'pw', split_axis=0, concat_axis=0, tiled=True)  8.3 us
    pallas_call x1, Pallas kernels, apply_planes(): pl.pallas_call(kernel, out_shape=jax.ShapeDtypeStruct((groups, 2 * rows,...  7.17 us
    pallas_call x1, Pallas kernels, spread_sticks(): pl.pallas_call(kernel, out_shape=jax.ShapeDtypeStruct((sizes.groups, 2 *...  1.99 us
    pallas_call x1, Pallas kernels, image_sticks(): pl.pallas_call(kernel, out_shape=(jax.ShapeDtypeStruct((height, local), f...  1.89 us
    another operation x2, other arithmetic, shards(): joined = jnp.stack([straight, turned], 1).reshape(4 * row_count, 2 * length)  1.5 us

commit v1 on v0

v1 whole, which is shorter than its diff:
```python
import math

import jax
import jax.numpy as jnp
import numpy as np
from jax import lax
from jax.experimental import pallas as pl
from jax.experimental.pallas import tpu as pltpu
from jax.sharding import PartitionSpec as P

kinetic_unit = 0.002
highest = lax.Precision.HIGHEST
lanes = 128
f32 = jnp.float32
bf16 = jnp.bfloat16


def round_up(count, step):
    return -(-count // step) * step


def signed_freq(index, grid_size):
    return jnp.where(index < grid_size // 2, index, index - grid_size)


def phases(out_index, in_index, direction, grid_size):
    angles = (out_index[:, None] * in_index[None, :]) % grid_size * (2.0 * math.pi / grid_size)
    cosine, sine = np.cos(angles), direction * np.sin(angles)
    return np.stack([np.stack([cosine, -sine], 1), np.stack([sine, cosine], 1)], 0)


def split(table, count):
    pieces = []
    rest = np.asarray(table, np.float64)
    for _ in range(count):
        piece = rest.astype(jnp.bfloat16)
        pieces.append(piece)
        rest = rest - piece.astype(np.float64)
    return pieces


class Sizes:
    def __init__(self, groups, planes, grid_size, stick_depth, sticks_local):
        self.groups, self.planes = groups, planes
        self.grid, self.depth, self.sticks_local = grid_size, stick_depth, sticks_local
        self.rows = round_up(planes, 16)
        self.sticks = groups * sticks_local
        self.box = round_up(2 * math.ceil(math.sqrt(self.sticks / math.pi)) + 2, 8)
        self.line = round_up(self.box, 64)
        self.low_count = max(1, 256 // self.line)
        self.high_count = self.box // self.low_count


def z_rows(sizes):
    group = np.repeat(np.arange(sizes.groups), sizes.rows)
    plane = np.tile(np.arange(sizes.rows), sizes.groups)
    return group * sizes.planes + plane, plane < sizes.planes


def z_back_table(sizes):
    z_freq = np.arange(sizes.depth) - sizes.depth // 2
    z_index, real = z_rows(sizes)
    table = phases(z_index, z_freq, 1, sizes.grid) * real[None, :, None, None]
    table = table.reshape(2, sizes.groups, sizes.rows, 2 * sizes.depth)
    high, low = split(table.transpose(1, 0, 2, 3).reshape(-1, 2 * sizes.depth), 2)
    return np.concatenate([high, low, high], 1)


def z_forward_table(sizes):
    z_freq = np.arange(sizes.depth) - sizes.depth // 2
    z_index, real = z_rows(sizes)
    table = phases(z_freq, z_index, -1, sizes.grid) * real / float(sizes.grid**3)
    table = table.reshape(2 * sizes.depth, 2, sizes.groups, sizes.rows)
    table = table.transpose(0, 2, 1, 3).reshape(2 * sizes.depth, -1)
    return np.concatenate(split(table, 3), 0)


def plane_tables(sizes):
    grid = np.arange(sizes.grid)
    y_freq = np.arange(sizes.line) - sizes.box // 2
    order = np.arange(sizes.box).reshape(sizes.high_count, sizes.low_count).T.reshape(-1)
    x_freq = order - sizes.box // 2
    inside = np.arange(sizes.line) < sizes.box
    y_back = phases(grid, y_freq, 1, sizes.grid) * inside
    y_back = y_back.reshape(2 * sizes.grid, -1).T
    y_forward = phases(y_freq, grid, -1, sizes.grid) * inside[None, :, None, None]
    y_forward = y_forward.reshape(-1, 2 * sizes.grid).T
    x_back = phases(grid, x_freq, 1, sizes.grid).reshape(2 * sizes.grid, -1)
    x_forward = phases(x_freq, grid, -1, sizes.grid).reshape(-1, 2 * sizes.grid)
    y_back = np.concatenate(split(y_back, 2), 0)
    x_high, x_low = split(x_back, 2)
    x_back = np.concatenate([x_high, x_low, x_high], 1)
    x_forward = np.concatenate(split(x_forward, 2), 0)
    y_forward = np.concatenate(split(y_forward, 2), 1)
    return y_back, x_back, x_forward, y_forward


def call_on_chip(kernel, name, operands, shapes, scratch=()):
    spec = pl.BlockSpec(memory_space=pltpu.VMEM)
    return pl.pallas_call(
        kernel,
        out_shape=tuple(pltpu.VMEM(shape, dtype) for shape, dtype in shapes),
        in_specs=[spec] * len(operands),
        out_specs=(spec,) * len(shapes),
        scratch_shapes=list(scratch),
        name=name,
    )(*[pltpu.with_memory_space_constraint(operand, pltpu.VMEM) for operand in operands])


def spread_sticks(sizes, vector, positions):
    block = 2 * sizes.rows

    def kernel(table_ref, vector_ref, position_ref, out_ref):
        vector = vector_ref[...]
        high = vector.astype(bf16)
        low = (vector - high.astype(f32)).astype(bf16)
        stacked = jnp.concatenate([high, high, low], 0)
        columns = jnp.dot(table_ref[...], stacked, preferred_element_type=f32)
        x_pos = (position_ref[...] // sizes.grid).astype(f32)
        y_pos = (position_ref[...] % sizes.grid).astype(f32)
        row = lax.broadcasted_iota(jnp.int32, (16, sizes.sticks_local), 0)
        tail = jnp.where(row == 0, x_pos, jnp.where(row == 1, y_pos, 0.0)).astype(bf16)
        for group in range(sizes.groups):
            out_ref[group, 0:block, :] = columns[group * block : (group + 1) * block].astype(bf16)
            out_ref[group, block:, :] = tail

    return call_on_chip(
        kernel,
        "spread_sticks",
        (jnp.asarray(z_back_table(sizes)), vector, positions[None, :]),
        (((sizes.groups, block + 16, sizes.sticks_local), bf16),),
    )[0]


def turn(position, size):
    angle = (position - 0.5 * size) * (2.0 * math.pi / size)
    square = angle * angle
    cosine = jnp.zeros_like(angle)
    sine = jnp.zeros_like(angle)
    for order in range(7, -1, -1):
        sign = (-1.0) ** order
        cosine = cosine * square + sign / math.factorial(2 * order)
        sine = sine * square + sign / math.factorial(2 * order + 1)
    return -cosine, -sine * angle


def anchor_of(position, grid_size):
    spot = lax.broadcasted_iota(jnp.int32, (1, grid_size), 1).astype(f32)

    def total(values):
        return jnp.sum(jnp.sum(values, axis=0, keepdims=True), axis=1, keepdims=True)

    cosine, sine = turn(position, grid_size)
    spot_cosine, spot_sine = turn(spot, grid_size)
    score = total(cosine) * spot_cosine + total(sine) * spot_sine
    best = jnp.max(score, axis=1, keepdims=True)
    return jnp.min(jnp.where(score >= best, spot, float(grid_size)), axis=1, keepdims=True)


def cross(first, second, line):
    if line % lanes == 0:
        count = first.shape[1] // line
        return [
            jnp.concatenate([side[:, i * line : (i + 1) * line] for side in (first, second)], 1) for i in range(count)
        ]
    low = lax.broadcasted_iota(jnp.int32, (first.shape[0], lanes), 1) < line
    results = []
    for start in range(0, first.shape[1], lanes):
        one, two = first[:, start : start + lanes], second[:, start : start + lanes]
        results.append(jnp.where(low, one, pltpu.roll(two, line, 1)))
        results.append(jnp.where(low, pltpu.roll(one, line, 1), two))
    return results


def apply_planes(sizes, received, potential):
    grid, box, line, rows = sizes.grid, sizes.box, sizes.line, sizes.rows
    groups, local, sticks = sizes.groups, sizes.sticks_local, sizes.sticks
    low_count, high_count = sizes.low_count, sizes.high_count
    columns = low_count * line
    half = high_count * rows

    def kernel(in_ref, pot_ref, yb_ref, xb_ref, xf_ref, yf_ref, out_ref, left_ref, hot_ref, a_ref, b_ref):
        def relative(row):
            position = jnp.concatenate([in_ref[g, 2 * rows : 2 * rows + 16, :].astype(f32)[row : row + 1] for g in range(groups)], 0)
            moved = position - anchor_of(position, grid) + float(box // 2)
            moved = jnp.where(moved < 0, moved + float(grid), moved)
            return jnp.where(moved >= float(grid), moved - float(grid), moved)

        x_rel, y_rel = relative(0), relative(1)
        x_high = jnp.floor(x_rel * (1.0 / low_count))
        column = (x_rel - x_high * low_count) * float(line) + y_rel
        step = lax.broadcasted_iota(jnp.int32, (16, local), 0).astype(f32).astype(bf16)
        highs = []
        for g in range(groups):
            where = slice(g * local, (g + 1) * local)
            column_here = jnp.broadcast_to(column[g : g + 1], (16, local)).astype(bf16)
            for start in range(0, columns, 16):
                hot_ref[start : start + 16, where] = jnp.where(
                    column_here == step + jnp.asarray(start, bf16), jnp.asarray(1, bf16), jnp.asarray(0, bf16)
                )
            highs.append(jnp.broadcast_to(x_high[g : g + 1], (rows, local)))
            high_here = highs[g].astype(bf16)
            for part in range(2):
                values = in_ref[g, part * rows : (part + 1) * rows, :]
                for high in range(high_count):
                    start = (part * high_count + high) * rows
                    left_ref[start : start + rows, where] = jnp.where(
                        high_here == jnp.asarray(high, bf16), values, jnp.asarray(0, bf16)
                    )

        placed = lax.dot_general(left_ref[...], hot_ref[...], (((1,), (1,)), ((), ())), preferred_element_type=f32)
        placed = jnp.concatenate(cross(placed[:half], placed[half:], line), 0).astype(bf16)
        lines = jnp.dot(jnp.concatenate([placed, placed], 1), yb_ref[...], preferred_element_type=f32)
        for part in range(2):
            a_ref[part] = lines[:, part * grid : (part + 1) * grid]

        def to_field(first):
            high, low = [], []
            for plane in (first, first + 1):
                lines = jnp.concatenate([a_ref[part, pl.ds(plane, box, stride=rows), :] for part in range(2)], 0)
                high.append(lines.astype(bf16))
                low.append((lines - high[-1].astype(f32)).astype(bf16))
            high, low = jnp.concatenate(high, 1), jnp.concatenate(low, 1)
            field = jnp.dot(xb_ref[...], jnp.concatenate([high, high, low], 0), preferred_element_type=f32)
            weight = jnp.concatenate([pot_ref[first], pot_ref[first + 1]], 1)
            return (field * jnp.concatenate([weight, weight], 0)).astype(bf16)

        def from_field(first, field):
            back = jnp.dot(xf_ref[...], field, preferred_element_type=f32)
            back = back[: 2 * box] + back[2 * box :]
            for index in range(2):
                for part in range(2):
                    b_ref[part, pl.ds(first + index, box, stride=rows), :] = back[
                        part * box : (part + 1) * box, index * grid : (index + 1) * grid
                    ]

        fields = [to_field(0)]
        for first in range(0, rows, 2):
            if first + 2 < rows:
                fields.append(to_field(first + 2))
            from_field(first, fields[first // 2])

        lines = jnp.concatenate([b_ref[0], b_ref[1]], 1).astype(bf16)
        boxed = jnp.dot(lines, yf_ref[...], preferred_element_type=f32)
        boxed = boxed[:, : 2 * line] + boxed[:, 2 * line :]
        if line % lanes == 0:
            parts = [
                jnp.concatenate([boxed[low * half : (low + 1) * half, part * line : (part + 1) * line] for low in range(low_count)], 1)
                for part in range(2)
            ]
        else:
            pairs = [
                cross(boxed[low * half : (low + 1) * half], boxed[(low + 1) * half : (low + 2) * half], line)
                for low in range(0, low_count, 2)
            ]
            parts = [jnp.concatenate([pair[part] for pair in pairs], 1) for part in range(2)]
        boxed = jnp.concatenate(parts, 0).astype(bf16)
        for first in range(0, groups, 2):
            found = jnp.dot(boxed, hot_ref[:, first * local : (first + 2) * local], preferred_element_type=f32)
            for g in (first, first + 1):
                for part in range(2):
                    total = jnp.zeros((rows, local), f32)
                    for high in range(high_count):
                        start = (part * high_count + high) * rows
                        piece = found[start : start + rows, (g - first) * local : (g - first + 1) * local]
                        total = total + jnp.where(highs[g] == float(high), piece, 0.0)
                    out_ref[g, part * rows : (part + 1) * rows, :] = total.astype(bf16)

    return call_on_chip(
        kernel,
        "apply_planes",
        (received, potential, *[jnp.asarray(t) for t in plane_tables(sizes)]),
        (((groups, 2 * rows, local), bf16),),
        (
            pltpu.VMEM((2 * half, sticks), bf16),
            pltpu.VMEM((columns, sticks), bf16),
            pltpu.VMEM((2, box * rows, grid), f32),
            pltpu.VMEM((2, box * rows, grid), f32),
        ),
    )[0]


def image_sticks(sizes, columns, vector, positions):
    depth, local, grid = sizes.depth, sizes.sticks_local, sizes.grid
    height = 2 * depth

    def kernel(table_ref, columns_ref, vector_ref, position_ref, image_ref, rounded_ref, sums_ref):
        product = jnp.dot(table_ref[...], columns_ref[...], preferred_element_type=f32)
        applied = product[:height] + (product[height : 2 * height] + product[2 * height :])
        vector = vector_ref[...]
        x_freq = signed_freq(position_ref[...] // grid, grid)
        y_freq = signed_freq(position_ref[...] % grid, grid)
        row = lax.broadcasted_iota(jnp.int32, (height, local), 0)
        z_freq = jnp.where(row < depth, row, row - depth) - depth // 2
        kinetic = kinetic_unit * (z_freq * z_freq + (x_freq * x_freq + y_freq * y_freq)).astype(f32)
        image = kinetic * vector + applied
        image_ref[...] = image
        rounded_ref[0:height, :] = vector.astype(bf16)
        rounded_ref[height:, :] = image.astype(bf16)
        sums_ref[0:1, :] = jnp.sum(vector * image, axis=0, keepdims=True)
        sums_ref[1:2, :] = jnp.sum(vector * vector, axis=0, keepdims=True)

    return call_on_chip(
        kernel,
        "image_sticks",
        (jnp.asarray(z_forward_table(sizes)), columns, vector, positions[None, :]),
        (((height, local), f32), ((2 * height, local), bf16), ((2, local), f32)),
    )


def finish(copies, image, vector, band, band_total, res_count):
    count = copies.shape[0]
    width = 2 * res_count
    table = np.zeros((width, width), np.float32)
    lane = np.arange(width)
    table[lane, lane % 2 * res_count + lane // 2] = 1.0

    def kernel(band_ref, table_ref, copies_ref, image_ref, vector_ref, residual_ref, ham_ref, inter_ref, total_ref):
        total = copies_ref[0]
        for index in range(1, count):
            total = total + copies_ref[index]
        tail = jnp.sum(total[4 * band_total : 4 * band_total + 2], axis=1, keepdims=True)
        residual_ref[...] = image_ref[...] - (tail[0:1] / tail[1:2]) * vector_ref[...]
        total_ref[...] = jnp.dot(total[: 4 * band_total], table_ref[...], precision=highest, preferred_element_type=f32)
        for column in range(band_total):
            source = column ^ band_ref[0]
            for index, out_ref in enumerate((inter_ref, ham_ref)):
                real = total_ref[pl.ds(source * 4 + index * 2, 1), :]
                imag = total_ref[pl.ds(source * 4 + index * 2 + 1, 1), :]
                out_ref[0, column : column + 1, :] = real[:, :res_count] + imag[:, res_count:]
                out_ref[1, column : column + 1, :] = imag[:, :res_count] - real[:, res_count:]

    spec = pl.BlockSpec(memory_space=pltpu.VMEM)
    operands = (jnp.asarray(table), copies, image, vector)
    projection = jax.ShapeDtypeStruct((2, band_total, res_count), f32)
    return pl.pallas_call(
        kernel,
        out_shape=(jax.ShapeDtypeStruct(image.shape, f32), projection, projection),
        in_specs=[pl.BlockSpec(memory_space=pltpu.SMEM)] + [spec] * 4,
        out_specs=(spec,) * 3,
        scratch_shapes=[pltpu.VMEM((4 * band_total, width), f32)],
        name="finish",
    )(band, *[pltpu.with_memory_space_constraint(operand, pltpu.VMEM) for operand in operands])


def shards(psi_res, correction, local_potential, stick_xy):
    groups, band_total = lax.axis_size("pw"), lax.axis_size("band")
    planes, grid_size = local_potential.shape[:2]
    _, _, stick_depth, sticks_local = correction.shape
    res_count = psi_res.shape[0]
    sizes = Sizes(groups, planes, grid_size, stick_depth, sticks_local)
    potential = jnp.pad(local_potential, ((0, sizes.rows - planes), (0, 0), (0, 0)))
    vector = correction.reshape(2 * stick_depth, sticks_local)

    moving = spread_sticks(sizes, vector, stick_xy)
    moving = lax.all_to_all(moving, "pw", split_axis=0, concat_axis=0, tiled=True)
    picked = apply_planes(sizes, moving, potential)
    picked = lax.all_to_all(picked, "pw", split_axis=0, concat_axis=0, tiled=True)
    picked = picked.reshape(2 * sizes.rows * groups, sticks_local)
    image, rounded, sums = image_sticks(sizes, picked, vector, stick_xy)

    blocks = [rounded] + [
        lax.ppermute(rounded, "band", [(i, i ^ step) for i in range(band_total)]) for step in range(1, band_total)
    ]
    joined = jnp.concatenate(blocks, 0).reshape(4 * band_total, stick_depth, sticks_local)
    product = lax.dot_general(
        joined,
        psi_res.reshape(2 * res_count, stick_depth, sticks_local),
        (((1, 2), (1, 2)), ((), ())),
        preferred_element_type=f32,
    )
    height = round_up(4 * band_total + 2, 8)
    fill = jnp.zeros((height - 4 * band_total - 2, sticks_local), f32)
    partial = jnp.concatenate([product, sums, fill], 0)
    copies = jnp.broadcast_to(partial[None], (groups,) + partial.shape)
    copies = lax.all_to_all(copies, "pw", split_axis=0, concat_axis=0, tiled=True)
    band = lax.axis_index("band")[None]
    residual, hamiltonian, intersection = finish(copies, image, vector, band, band_total, res_count)
    return (
        residual.reshape(correction.shape),
        jnp.transpose(hamiltonian, (0, 2, 1)),
        jnp.transpose(intersection, (0, 2, 1)),
    )


def solution(mesh):
    return jax.shard_map(
        shards,
        mesh=mesh,
        in_specs=(
            P("band", None, None, "pw"),
            P("band", None, None, "pw"),
            P("pw", None, None),
            P("pw"),
        ),
        out_specs=(P("band", None, None, "pw"), P(None, "band", None), P(None, "band", None)),
        check_vma=False,
    )
```

time: 59.3 us -> 54.9 us (0.926)
  blocking collectives: 40.4 us -> 20.9 us
  waiting for transfers between devices: 0 us -> 10.9 us
  starting transfers between devices: 0 us -> 6.91 us
  Pallas kernels: 11.1 us -> 4.32 us
  local copies, waits for them, and re-layouts: 1.81 us -> 8.09 us
  other arithmetic: 2.82 us -> 0.1 us
  matrix products: 0.72 us -> 2.37 us
  between operations: 2.04 us -> 0.7 us
    all_gather x1 -> x0, blocking collectives: 9.44 us -> none  [shards(): rows = lax.all_gather(rounded, 'band', axis=0, tiled=True)]
    all_to_all x1 -> x0, blocking collectives: 8.3 us -> none  [shards(): lax.all_to_all(copies, 'pw', split_axis=0, concat_axis=0, tiled=True)]
    unnamed x9 -> x24, local copies, waits for them, and re-layouts: 0.12 us -> 7.33 us
    pallas_call x3 -> x4, Pallas kernels: 11.1 us -> 4.32 us  [the longest x3 3.46 us: call_on_chip(): pl.pallas_call(kernel, out_shape=tuple((pltpu.VMEM(shape, dtype) for shap...]
    all_to_all x0 -> x1, waiting for transfers between devices: none -> 6.24 us  [shards(): lax.all_to_all(copies, 'pw', split_axis=0, concat_axis=0, tiled=True)]
    ppermute x0 -> x3, waiting for transfers between devices: none -> 4.69 us  [shards(): lax.ppermute(rounded, 'band', [(i, i ^ step) for i in range(band_total)])]
    ppermute x0 -> x3, starting transfers between devices: none -> 3.55 us  [shards(): lax.ppermute(rounded, 'band', [(i, i ^ step) for i in range(band_total)])]
    all_to_all x0 -> x1, starting transfers between devices: none -> 3.36 us  [shards(): lax.all_to_all(copies, 'pw', split_axis=0, concat_axis=0, tiled=True)]
  transfers between devices with their start and end apart: 0 -> 4, of which waited for: 0 -> 4; matrix products, arithmetic and copies ran while one was open for 0% -> 0% of each run, Pallas kernels for 0% -> 0%
where the time goes in v1:
time: 54.9 us; the launch traced here: 54.3 us
  blocking collectives  20.9 us (38%)
  waiting for transfers between devices  10.9 us (20%)
  local copies, waits for them, and re-layouts  8.09 us (15%)
  starting transfers between devices  6.91 us (13%)
  Pallas kernels  4.32 us (8%)
  matrix products  2.37 us (4%)
  between operations  0.7 us (1%)
    all_to_all x1, blocking collectives, shards(): lax.all_to_all(moving, 'pw', split_axis=0, concat_axis=0, tiled=True)  12.5 us
    all_to_all x1, blocking collectives, shards(): lax.all_to_all(picked, 'pw', split_axis=0, concat_axis=0, tiled=True)  8.43 us
    unnamed x24, local copies, waits for them, and re-layouts  7.33 us
    all_to_all x1, waiting for transfers between devices, shards(): lax.all_to_all(copies, 'pw', split_axis=0, concat_axis=0, tiled=True)  6.24 us
    ppermute x3, waiting for transfers between devices, shards(): lax.ppermute(rounded, 'band', [(i, i ^ step) for i in range(band_total)])  4.69 us
    ppermute x3, starting transfers between devices, shards(): lax.ppermute(rounded, 'band', [(i, i ^ step) for i in range(band_total)])  3.55 us
    pallas_call x3, Pallas kernels, call_on_chip(): pl.pallas_call(kernel, out_shape=tuple((pltpu.VMEM(shape, dtype) for shap...  3.46 us
    all_to_all x1, starting transfers between devices, shards(): lax.all_to_all(copies, 'pw', split_axis=0, concat_axis=0, tiled=True)  3.36 us
  transfers between devices with their start and end apart: 4, of which 4 were waited for; matrix products, arithmetic and copies ran while one was open for 0% of the time, Pallas kernels for 0%

profile of v1, /device:TPU:0, one launch (start us, length us, event | category | flops | bytes accessed | tf_op | source)
XLA Modules:
  0.0 54.3 jit_solution(7890240179317039008)
XLA Ops:
  0.6 0.0 copy-start.11
  0.6 0.0 copy-start.1
  0.7 0.9 %copy-done.1 = f32[1,2,72,128]{3,2,1,0:T(8,128)S(1)} copy-done((f32[1,2,72,128]{3,2,1,0:T(8,128)S(1)}, f32[1,2,72,128]{3,2,1,0:T(8,128)}, u32[]{:S(2)}) %copy-start.1) | copy-done | bytes 73752
  1.5 0.9 %copy-done.3 = bf16[256,432]{1,0:T(8,128)(2,1)S(1)} copy-done((bf16[256,432]{1,0:T(8,128)(2,1)S(1)}, bf16[256,432]{1,0:T(8,128)(2,1)}, u32[]{:S(2)}) %copy-start.3) | copy-done | bytes 221208
  2.5 0.7 %copy-done.10 = s32[128]{0:T(128)S(1)} copy-done((s32[128]{0:T(128)S(1)}, s32[128]{0:T(128)}, u32[]{:S(2)}) %copy-start.10) | copy-done | bytes 536
  3.1 0.2 spread_sticks.1
  3.4 12.5 %all_to_all.15.in_ref = bf16[8,48,128]{2,1,0:T(8,128)(2,1)S(1)} all-to-all(bf16[8,48,128]{2,1,0:T(8,128)(2,1)S(1)} %spread_sticks.1), channel_id=1, replica_groups=mesh['pw'=8,'band'=4] {'pw'}, dimensions={0} | all-to-all | bytes 196608 | tf_op jit(solution)/shard_map/all_to_all | solution.py:356
  15.8 1.2 %copy-done = f32[16,128,128]{2,1,0:T(8,128)S(1)} copy-done((f32[16,128,128]{2,1,0:T(8,128)S(1)}, f32[16,128,128]{2,1,0:T(8,128)}, u32[]{:S(2)}) %copy-start) | copy-done | bytes 1048600
  17.1 0.9 %copy-done.5 = bf16[256,256]{1,0:T(8,128)(2,1)S(1)} copy-done((bf16[256,256]{1,0:T(8,128)(2,1)S(1)}, bf16[256,256]{1,0:T(8,128)(2,1)}, u32[]{:S(2)}) %copy-start.5) | copy-done | bytes 131096
  18.0 0.9 %copy-done.6 = bf16[256,240]{1,0:T(8,128)(2,1)S(1)} copy-done((bf16[256,240]{1,0:T(8,128)(2,1)S(1)}, bf16[256,240]{1,0:T(8,128)(2,1)}, u32[]{:S(2)}) %copy-start.6) | copy-done | bytes 122904
  18.9 0.9 %copy-done.7 = bf16[256,256]{1,0:T(8,128)(2,1)S(1)} copy-done((bf16[256,256]{1,0:T(8,128)(2,1)S(1)}, bf16[256,256]{1,0:T(8,128)(2,1)}, u32[]{:S(2)}) %copy-start.7) | copy-done | bytes 131096
  19.8 0.9 %copy-done.8 = bf16[160,256]{1,0:T(8,128)(2,1)S(1)} copy-done((bf16[160,256]{1,0:T(8,128)(2,1)S(1)}, bf16[160,256]{1,0:T(8,128)(2,1)}, u32[]{:S(2)}) %copy-start.8) | copy-done | bytes 81944
  20.7 3.0 %apply_planes.1 = bf16[8,32,128]{2,1,0:T(8,128)(2,1)S(1)} custom-call(bf16[8,48,128]{2,1,0:T(8,128)(2,1)S(1)} %all_to_all.15.in_ref, f32[16,128,128]{2,1,0:T(8,128)S(1)} %copy-done, bf16[256,256]{1,0:T(8,128)(2,1)S(1)} %copy-done.5, bf16[256,240]{1,0:T(8,128)(2,1)S(1)} %copy-done.6, bf16[160,256]{1,0:T(8,128)(2,1)S(1)} %copy-done.8, ...), custom_call_target="tpu_custom_call" | custom-call | tf_op jit(solution)/shard_map/apply_planes/pallas_call | solution.py:100
  23.7 0.0 copy-start.9
  23.7 8.4 %all_to_all.16 = bf16[8,32,128]{2,1,0:T(8,128)(2,1)S(1)} all-to-all(bf16[8,32,128]{2,1,0:T(8,128)(2,1)S(1)} %apply_planes.1), channel_id=1, replica_groups=mesh['pw'=8,'band'=4] {'pw'}, dimensions={0} | all-to-all | bytes 131072 | tf_op jit(solution)/shard_map/all_to_all | solution.py:358
  32.1 0.0 copy-done.11
  32.1 0.0 copy-done.2
  32.1 0.2 image_sticks.1
  32.4 1.6 %collective-permute-start = (bf16[288,128]{1,0:T(8,128)(2,1)S(1)}, bf16[288,128]{1,0:T(8,128)(2,1)S(1)}, u32[]{:S(2)}, u32[]{:S(2)}) collective-permute-start(bf16[288,128]{1,0:T(8,128)(2,1)S(1)} %get-tuple-element.9), channel_id=1, source_target_pairs={{0,1},{1,0},{2,3},{3,2},{4,5},{5,4},{6,7},{7,6},{8,9},{9,8},{10,11... | collective-permute-start | bytes 221192 | tf_op jit(solution)/shard_map/ppermute | solution.py:363
  33.9 1.5 %collective-permute-start.1 = (bf16[288,128]{1,0:T(8,128)(2,1)S(1)}, bf16[288,128]{1,0:T(8,128)(2,1)S(1)}, u32[]{:S(2)}, u32[]{:S(2)}) collective-permute-start(bf16[288,128]{1,0:T(8,128)(2,1)S(1)} %get-tuple-element.9), channel_id=1, source_target_pairs={{0,2},{1,3},{2,0},{3,1},{4,6},{5,7},{6,4},{7,5},{8,10},{9,11},{10,... | collective-permute-start | bytes 221192 | tf_op jit(solution)/shard_map/ppermute | solution.py:363
  35.4 0.5 collective-permute-start.2
  35.9 0.1 pad.2.clone
  36.0 0.8 %collective-permute-done = bf16[288,128]{1,0:T(8,128)(2,1)S(1)} collective-permute-done((bf16[288,128]{1,0:T(8,128)(2,1)S(1)}, bf16[288,128]{1,0:T(8,128)(2,1)S(1)}, u32[]{:S(2)}, u32[]{:S(2)}) %collective-permute-start) | collective-permute-done | bytes 73760 | tf_op jit(solution)/shard_map/ppermute | solution.py:363
  36.8 2.3 %collective-permute-done.1 = bf16[288,128]{1,0:T(8,128)(2,1)S(1)} collective-permute-done((bf16[288,128]{1,0:T(8,128)(2,1)S(1)}, bf16[288,128]{1,0:T(8,128)(2,1)S(1)}, u32[]{:S(2)}, u32[]{:S(2)}) %collective-permute-start.1) | collective-permute-done | bytes 73760 | tf_op jit(solution)/shard_map/ppermute | solution.py:363
  39.1 1.6 %collective-permute-done.2 = bf16[288,128]{1,0:T(8,128)(2,1)S(1)} collective-permute-done((bf16[288,128]{1,0:T(8,128)(2,1)S(1)}, bf16[288,128]{1,0:T(8,128)(2,1)S(1)}, u32[]{:S(2)}, u32[]{:S(2)}) %collective-permute-start.2) | collective-permute-done | bytes 73760 | tf_op jit(solution)/shard_map/ppermute | solution.py:363
  40.7 2.4 %fusion.2 = f32[16,128]{1,0:T(8,128)S(1)} fusion(bf16[128,72,128]{2,1,0:T(8,128)(2,1)} %bitcast.18, bf16[16,72,128]{2,1,0:T(8,128)(2,1)S(1)} %bitcast.17), kind=kOutput, calls=%fused_computation.2 | convolution fusion | flops 37748736 | bytes 2662400 | tf_op jit(solution)/shard_map/dot_general | solution.py:366
  43.1 0.1 maximum_maximum_fusion
  43.2 0.7 %broadcast_in_dim.19 = f32[8,24,128]{2,1,0:T(8,128)} broadcast(f32[24,128]{1,0:T(8,128)S(1)} %maximum_maximum_fusion), dimensions={1,2} | broadcast | bytes 110592 | tf_op jit(solution)/shard_map/broadcast_in_dim | solution.py:375
  43.8 3.4 %all-to-all-start.2 = ((f32[8,24,128]{2,1,0:T(8,128)}), f32[8,24,128]{2,1,0:T(8,128)S(1)}, u32[]{:S(2)}, u32[]{:S(2)}) async-start(f32[8,24,128]{2,1,0:T(8,128)} %broadcast_in_dim.19), calls=%async_computation.2 | async-start | bytes 196608 | tf_op jit(solution)/shard_map/all_to_all | solution.py:376
  47.2 6.2 %all-to-all-done.2.copies_ref = f32[8,24,128]{2,1,0:T(8,128)S(1)} async-done(((f32[8,24,128]{2,1,0:T(8,128)}), f32[8,24,128]{2,1,0:T(8,128)S(1)}, u32[]{:S(2)}, u32[]{:S(2)}) %all-to-all-start.2) | async-done | bytes 98336 | tf_op jit(solution)/shard_map/all_to_all | solution.py:376
  53.4 0.0 copy-done.9
  53.4 0.9 %finish.1 = (f32[144,128]{1,0:T(8,128)}, f32[2,4,64]{2,1,0:T(4,128)}, f32[2,4,64]{2,1,0:T(4,128)}) custom-call(s32[1]{0:T(128)} %bitcast.band_ref, f32[128,128]{1,0:T(8,128)S(1)} %copy-done.9, f32[8,24,128]{2,1,0:T(8,128)S(1)} %all-to-all-done.2.copies_ref, f32[144,128]{1,0:T(8,128)S(1)} %get-tuple-element.11.image_ref, f32[144,128]{1,0:T(8,128)S(1)} %bitcast.13), custom_call_target="tpu_custom_call" | custom-call | tf_op jit(solution)/shard_map/finish/pallas_call | solution.py:336
  (12 shorter events, 0.0 us)
Async XLA Ops:
  0.6 31.5 %copy-start.11 = (s32[128]{0:T(128)S(1)}, s32[128]{0:T(128)}, u32[]{:S(2)}) copy-start(s32[128]{0:T(128)} %param.14) | copy-start | bytes 1540
  0.6 0.9 %copy-start.1 = (f32[1,2,72,128]{3,2,1,0:T(8,128)S(1)}, f32[1,2,72,128]{3,2,1,0:T(8,128)}, u32[]{:S(2)}) copy-start(f32[1,2,72,128]{3,2,1,0:T(8,128)} %param.12) | copy-start | bytes 221188
  1.5 0.9 %copy-start.3 = (bf16[256,432]{1,0:T(8,128)(2,1)S(1)}, bf16[256,432]{1,0:T(8,128)(2,1)}, u32[]{:S(2)}) copy-start(bf16[256,432]{1,0:T(8,128)(2,1)} %constant.8.clone.table_ref) | copy-start | bytes 663556
  2.5 0.7 %copy-start.10 = (s32[128]{0:T(128)S(1)}, s32[128]{0:T(128)}, u32[]{:S(2)}) copy-start(s32[128]{0:T(128)} %param.14) | copy-start | bytes 1540
  3.1 29.0 %copy-start.2 = (f32[1,2,72,128]{3,2,1,0:T(8,128)S(1)}, f32[1,2,72,128]{3,2,1,0:T(8,128)}, u32[]{:S(2)}) copy-start(f32[1,2,72,128]{3,2,1,0:T(8,128)} %param.12) | copy-start | bytes 221188
  3.1 29.0 %copy-start.4 = (bf16[432,256]{1,0:T(8,128)(2,1)S(1)}, bf16[432,256]{1,0:T(8,128)(2,1)}, u32[]{:S(2)}) copy-start(bf16[432,256]{1,0:T(8,128)(2,1)} %constant.26.clone.table_ref) | copy-start | bytes 663556
  15.8 1.2 %copy-start = (f32[16,128,128]{2,1,0:T(8,128)S(1)}, f32[16,128,128]{2,1,0:T(8,128)}, u32[]{:S(2)}) copy-start(f32[16,128,128]{2,1,0:T(8,128)} %pot_ref.1) | copy-start | bytes 3145732
  17.1 0.9 %copy-start.5 = (bf16[256,256]{1,0:T(8,128)(2,1)S(1)}, bf16[256,256]{1,0:T(8,128)(2,1)}, u32[]{:S(2)}) copy-start(bf16[256,256]{1,0:T(8,128)(2,1)} %constant.22.clone.yb_ref) | copy-start | bytes 393220
  18.0 0.9 %copy-start.6 = (bf16[256,240]{1,0:T(8,128)(2,1)S(1)}, bf16[256,240]{1,0:T(8,128)(2,1)}, u32[]{:S(2)}) copy-start(bf16[256,240]{1,0:T(8,128)(2,1)} %constant.23.clone.xb_ref) | copy-start | bytes 368644
  18.9 0.9 %copy-start.7 = (bf16[256,256]{1,0:T(8,128)(2,1)S(1)}, bf16[256,256]{1,0:T(8,128)(2,1)}, u32[]{:S(2)}) copy-start(bf16[256,256]{1,0:T(8,128)(2,1)} %constant.25.clone.yf_ref) | copy-start | bytes 393220
  19.8 0.9 %copy-start.8 = (bf16[160,256]{1,0:T(8,128)(2,1)S(1)}, bf16[160,256]{1,0:T(8,128)(2,1)}, u32[]{:S(2)}) copy-start(bf16[160,256]{1,0:T(8,128)(2,1)} %constant.24.clone.xf_ref) | copy-start | bytes 245764
  23.7 29.8 %copy-start.9 = (f32[128,128]{1,0:T(8,128)S(1)}, f32[128,128]{1,0:T(8,128)}, u32[]{:S(2)}) copy-start(f32[128,128]{1,0:T(8,128)} %constant.27.clone.table_ref) | copy-start | bytes 196612
  32.4 4.4 %collective-permute-start = (bf16[288,128]{1,0:T(8,128)(2,1)S(1)}, bf16[288,128]{1,0:T(8,128)(2,1)S(1)}, u32[]{:S(2)}, u32[]{:S(2)}) collective-permute-start(bf16[288,128]{1,0:T(8,128)(2,1)S(1)} %get-tuple-element.9), channel_id=1, source_target_pairs={{0,1},{1,0},{2,3},{3,2},{4,5},{5,4},{6,7},{7,6},{8,9},{9,8},{10,11... | collective-permute-start | bytes 221192 | tf_op jit(solution)/shard_map/ppermute | solution.py:363
  33.9 5.1 %collective-permute-start.1 = (bf16[288,128]{1,0:T(8,128)(2,1)S(1)}, bf16[288,128]{1,0:T(8,128)(2,1)S(1)}, u32[]{:S(2)}, u32[]{:S(2)}) collective-permute-start(bf16[288,128]{1,0:T(8,128)(2,1)S(1)} %get-tuple-element.9), channel_id=1, source_target_pairs={{0,2},{1,3},{2,0},{3,1},{4,6},{5,7},{6,4},{7,5},{8,10},{9,11},{10,... | collective-permute-start | bytes 221192 | tf_op jit(solution)/shard_map/ppermute | solution.py:363
  35.4 5.3 %collective-permute-start.2 = (bf16[288,128]{1,0:T(8,128)(2,1)S(1)}, bf16[288,128]{1,0:T(8,128)(2,1)S(1)}, u32[]{:S(2)}, u32[]{:S(2)}) collective-permute-start(bf16[288,128]{1,0:T(8,128)(2,1)S(1)} %get-tuple-element.9), channel_id=1, source_target_pairs={{0,3},{1,2},{2,1},{3,0},{4,7},{5,6},{6,5},{7,4},{8,11},{9,10},{10,... | collective-permute-start | bytes 221192 | tf_op jit(solution)/shard_map/ppermute | solution.py:363
  43.8 9.6 %all-to-all-start.2 = ((f32[8,24,128]{2,1,0:T(8,128)}), f32[8,24,128]{2,1,0:T(8,128)S(1)}, u32[]{:S(2)}, u32[]{:S(2)}) async-start(f32[8,24,128]{2,1,0:T(8,128)} %broadcast_in_dim.19), calls=%async_computation.2 | async-start | bytes 196608 | tf_op jit(solution)/shard_map/all_to_all | solution.py:376

commit v2 on v1

--- a/solution.py
+++ b/solution.py
@@ -95,22 +95,29 @@
     return y_back, x_back, x_forward, y_forward
 
 
-def call_on_chip(kernel, name, operands, shapes, scratch=()):
+def call_on_chip(kernel, name, operands, shapes, far=(), scratch=()):
     spec = pl.BlockSpec(memory_space=pltpu.VMEM)
     return pl.pallas_call(
         kernel,
         out_shape=tuple(pltpu.VMEM(shape, dtype) for shape, dtype in shapes),
-        in_specs=[spec] * len(operands),
+        in_specs=[spec] * len(operands) + [pl.BlockSpec(memory_space=pl.ANY)] * len(far),
         out_specs=(spec,) * len(shapes),
         scratch_shapes=list(scratch),
         name=name,
-    )(*[pltpu.with_memory_space_constraint(operand, pltpu.VMEM) for operand in operands])
+    )(*[pltpu.with_memory_space_constraint(operand, pltpu.VMEM) for operand in operands], *far)
 
 
 def spread_sticks(sizes, vector, positions):
     block = 2 * sizes.rows
-
-    def kernel(table_ref, vector_ref, position_ref, out_ref):
+    far = (jnp.asarray(z_back_table(sizes)), vector, positions[None, :])
+
+    def kernel(table_far, vector_far, position_far, out_ref, table_ref, vector_ref, position_ref, sems):
+        pairs = ((vector_far, vector_ref), (table_far, table_ref), (position_far, position_ref))
+        copies = [pltpu.make_async_copy(far, near, sems.at[index]) for index, (far, near) in enumerate(pairs)]
+        for copy in copies:
+            copy.start()
+        for copy in copies:
+            copy.wait()
         vector = vector_ref[...]
         high = vector.astype(bf16)
         low = (vector - high.astype(f32)).astype(bf16)
@@ -127,8 +134,10 @@
     return call_on_chip(
         kernel,
         "spread_sticks",
-        (jnp.asarray(z_back_table(sizes)), vector, positions[None, :]),
+        (),
         (((sizes.groups, block + 16, sizes.sticks_local), bf16),),
+        far,
+        [pltpu.VMEM(operand.shape, operand.dtype) for operand in far] + [pltpu.SemaphoreType.DMA((3,))],
     )[0]
 
 
@@ -172,14 +181,26 @@
     return results
 
 
-def apply_planes(sizes, received, potential):
+def apply_planes(sizes, received, potential, psi_res):
+    far = (*[jnp.asarray(t) for t in plane_tables(sizes)], potential, psi_res)
     grid, box, line, rows = sizes.grid, sizes.box, sizes.line, sizes.rows
     groups, local, sticks = sizes.groups, sizes.sticks_local, sizes.sticks
     low_count, high_count = sizes.low_count, sizes.high_count
     columns = low_count * line
     half = high_count * rows
 
-    def kernel(in_ref, pot_ref, yb_ref, xb_ref, xf_ref, yf_ref, out_ref, left_ref, hot_ref, a_ref, b_ref):
+    def kernel(in_ref, *refs):
+        distant, (out_ref, psi_ref), near = refs[:6], refs[6:8], refs[8:13]
+        left_ref, hot_ref, a_ref, b_ref, sems = refs[13:]
+        yb_ref, xb_ref, xf_ref, yf_ref, pot_ref = near
+        copies = [
+            pltpu.make_async_copy(source, target, sems.at[index])
+            for index, (source, target) in enumerate(zip(distant, (*near, psi_ref), strict=True))
+        ]
+        yb_copy, xb_copy, xf_copy, yf_copy, pot_copy, psi_copy = copies
+        for copy in copies:
+            copy.start()
+
         def relative(row):
             position = jnp.concatenate([in_ref[g, 2 * rows : 2 * rows + 16, :].astype(f32)[row : row + 1] for g in range(groups)], 0)
             moved = position - anchor_of(position, grid) + float(box // 2)
@@ -209,6 +230,7 @@
                     )
 
         placed = lax.dot_general(left_ref[...], hot_ref[...], (((1,), (1,)), ((), ())), preferred_element_type=f32)
+        yb_copy.wait()
         placed = jnp.concatenate(cross(placed[:half], placed[half:], line), 0).astype(bf16)
         lines = jnp.dot(jnp.concatenate([placed, placed], 1), yb_ref[...], preferred_element_type=f32)
         for part in range(2):
@@ -234,12 +256,15 @@
                         part * box : (part + 1) * box, index * grid : (index + 1) * grid
                     ]
 
+        for copy in (xb_copy, pot_copy, xf_copy):
+            copy.wait()
         fields = [to_field(0)]
         for first in range(0, rows, 2):
             if first + 2 < rows:
                 fields.append(to_field(first + 2))
             from_field(first, fields[first // 2])
 
+        yf_copy.wait()
         lines = jnp.concatenate([b_ref[0], b_ref[1]], 1).astype(bf16)
         boxed = jnp.dot(lines, yf_ref[...], preferred_element_type=f32)
         boxed = boxed[:, : 2 * line] + boxed[:, 2 * line :]
@@ -265,19 +290,23 @@
                         piece = found[start : start + rows, (g - first) * local : (g - first + 1) * local]
                         total = total + jnp.where(highs[g] == float(high), piece, 0.0)
                     out_ref[g, part * rows : (part + 1) * rows, :] = total.astype(bf16)
+        psi_copy.wait()
 
     return call_on_chip(
         kernel,
         "apply_planes",
-        (received, potential, *[jnp.asarray(t) for t in plane_tables(sizes)]),
-        (((groups, 2 * rows, local), bf16),),
+        (received,),
+        (((groups, 2 * rows, local), bf16), (psi_res.shape, psi_res.dtype)),
+        far,
         (
+            *[pltpu.VMEM(operand.shape, operand.dtype) for operand in far[:5]],
             pltpu.VMEM((2 * half, sticks), bf16),
             pltpu.VMEM((columns, sticks), bf16),
             pltpu.VMEM((2, box * rows, grid), f32),
             pltpu.VMEM((2, box * rows, grid), f32),
+            pltpu.SemaphoreType.DMA((6,)),
         ),
-    )[0]
+    )
 
 
 def image_sticks(sizes, columns, vector, positions):
@@ -308,6 +337,19 @@
     )
 
 
+def share(product, sums, groups):
+    count, width = product.shape
+    height = round_up(count + 2, 8)
+
+    def kernel(product_ref, sums_ref, out_ref):
+        fill = jnp.zeros((height - count - 2, width), f32)
+        partial = jnp.concatenate([product_ref[...], sums_ref[...], fill], 0)
+        for group in range(groups):
+            out_ref[group] = partial
+
+    return call_on_chip(kernel, "share", (product, sums), (((groups, height, width), f32),))[0]
+
+
 def finish(copies, image, vector, band, band_total, res_count):
     count = copies.shape[0]
     width = 2 * res_count
@@ -354,7 +396,7 @@
 
     moving = spread_sticks(sizes, vector, stick_xy)
     moving = lax.all_to_all(moving, "pw", split_axis=0, concat_axis=0, tiled=True)
-    picked = apply_planes(sizes, moving, potential)
+    picked, psi_near = apply_planes(sizes, moving, potential, psi_res.reshape(2 * res_count, stick_depth, sticks_local))
     picked = lax.all_to_all(picked, "pw", split_axis=0, concat_axis=0, tiled=True)
     picked = picked.reshape(2 * sizes.rows * groups, sticks_local)
     image, rounded, sums = image_sticks(sizes, picked, vector, stick_xy)
@@ -365,14 +407,11 @@
     joined = jnp.concatenate(blocks, 0).reshape(4 * band_total, stick_depth, sticks_local)
     product = lax.dot_general(
         joined,
-        psi_res.reshape(2 * res_count, stick_depth, sticks_local),
+        psi_near,
         (((1, 2), (1, 2)), ((), ())),
         preferred_element_type=f32,
     )
-    height = round_up(4 * band_total + 2, 8)
-    fill = jnp.zeros((height - 4 * band_total - 2, sticks_local), f32)
-    partial = jnp.concatenate([product, sums, fill], 0)
-    copies = jnp.broadcast_to(partial[None], (groups,) + partial.shape)
+    copies = share(product, sums, groups)
     copies = lax.all_to_all(copies, "pw", split_axis=0, concat_axis=0, tiled=True)
     band = lax.axis_index("band")[None]
     residual, hamiltonian, intersection = finish(copies, image, vector, band, band_total, res_count)

time: 54.9 us -> 47.6 us (0.87)
  local copies, waits for them, and re-layouts: 8.09 us -> 0.02 us
  Pallas kernels: 4.32 us -> 6.98 us
  matrix products: 2.37 us -> 0.7 us
    unnamed x24 -> x8, local copies, waits for them, and re-layouts: 7.33 us -> 0.02 us
    pallas_call x3 -> x4, Pallas kernels: 3.46 us -> 6.12 us  [call_on_chip(): pl.pallas_call(kernel, out_shape=tuple((pltpu.VMEM(shape, dtype) for shap...]
    dot_general x1, matrix products: 2.37 us -> 0.7 us  [shards(): lax.dot_general(joined, psi_near, (((1, 2), (1, 2)), ((), ())), preferred...]
    broadcast_in_dim x2 -> x0, local copies, waits for them, and re-layouts: 0.68 us -> none  [the longest x1 0.68 us: shards(): copies = jnp.broadcast_to(partial[None], (groups,) + partial.shape)]
where the time goes in v2:
time: 47.6 us; the launch traced here: 47.3 us
  blocking collectives  20.9 us (44%)
  waiting for transfers between devices  11 us (23%)
  Pallas kernels  6.98 us (15%)
  starting transfers between devices  6.91 us (15%)
  matrix products  0.7 us (1%)
  between operations  0.7 us (1%)
    all_to_all x1, blocking collectives, shards(): lax.all_to_all(moving, 'pw', split_axis=0, concat_axis=0, tiled=True)  12.5 us
    all_to_all x1, blocking collectives, shards(): lax.all_to_all(picked, 'pw', split_axis=0, concat_axis=0, tiled=True)  8.43 us
    all_to_all x1, waiting for transfers between devices, shards(): lax.all_to_all(copies, 'pw', split_axis=0, concat_axis=0, tiled=True)  6.24 us
    pallas_call x4, Pallas kernels, call_on_chip(): pl.pallas_call(kernel, out_shape=tuple((pltpu.VMEM(shape, dtype) for shap...  6.12 us
    ppermute x3, waiting for transfers between devices, shards(): lax.ppermute(rounded, 'band', [(i, i ^ step) for i in range(band_total)])  4.78 us
    ppermute x3, starting transfers between devices, shards(): lax.ppermute(rounded, 'band', [(i, i ^ step) for i in range(band_total)])  3.55 us
    all_to_all x1, starting transfers between devices, shards(): lax.all_to_all(copies, 'pw', split_axis=0, concat_axis=0, tiled=True)  3.36 us
  transfers between devices with their start and end apart: 4, of which 4 were waited for; matrix products, arithmetic and copies ran while one was open for 0% of the time, Pallas kernels for 0%

profile of v2, /device:TPU:0, one launch (start us, length us, event | category | flops | bytes accessed | tf_op | source)
XLA Modules:
  0.0 47.3 jit_solution(6401293197507413569)
XLA Ops:
  0.6 0.0 copy-start
  0.6 0.0 copy-start.1
  0.7 0.0 copy-start.3
  0.7 1.3 %spread_sticks.1 = bf16[8,48,128]{2,1,0:T(8,128)(2,1)S(1)} custom-call(bf16[256,432]{1,0:T(8,128)(2,1)} %constant.9.clone.table_far, f32[144,128]{1,0:T(8,128)} %bitcast.11, s32[1,128]{1,0:T(1,128)} %bitcast.15), custom_call_target="tpu_custom_call" | custom-call | tf_op jit(solution)/shard_map/spread_sticks/pallas_call | solution.py:100
  2.0 12.5 %all_to_all.15.in_ref = bf16[8,48,128]{2,1,0:T(8,128)(2,1)S(1)} all-to-all(bf16[8,48,128]{2,1,0:T(8,128)(2,1)S(1)} %spread_sticks.1), channel_id=1, replica_groups=mesh['pw'=8,'band'=4] {'pw'}, dimensions={0} | all-to-all | bytes 196608 | tf_op jit(solution)/shard_map/all_to_all | solution.py:398
  14.4 3.9 %apply_planes.1 = (bf16[8,32,128]{2,1,0:T(8,128)(2,1)S(1)}, bf16[128,72,128]{2,1,0:T(8,128)(2,1)S(1)}) custom-call(bf16[8,48,128]{2,1,0:T(8,128)(2,1)S(1)} %all_to_all.15.in_ref, bf16[256,256]{1,0:T(8,128)(2,1)} %constant.20.clone.refs_0_, bf16[256,240]{1,0:T(8,128)(2,1)} %constant.21.clone.refs_1_, bf16[160,256]{1,0:T(8,128)(2,1)} %constant.22.clone.refs_2_, ...), custom_call_target="tpu_custom_call" | custom-call | tf_op jit(solution)/shard_map/apply_planes/pallas_call | solution.py:100
  18.4 0.0 copy-start.2
  18.4 8.4 %all_to_all.16 = bf16[8,32,128]{2,1,0:T(8,128)(2,1)S(1)} all-to-all(bf16[8,32,128]{2,1,0:T(8,128)(2,1)S(1)} %get-tuple-element.11), channel_id=1, replica_groups=mesh['pw'=8,'band'=4] {'pw'}, dimensions={0} | all-to-all | bytes 131072 | tf_op jit(solution)/shard_map/all_to_all | solution.py:400
  26.8 0.0 copy-done
  26.8 0.0 copy-done.1
  26.8 0.0 copy-done.3
  26.8 0.2 image_sticks.1
  27.0 1.6 %collective-permute-start = (bf16[288,128]{1,0:T(8,128)(2,1)S(1)}, bf16[288,128]{1,0:T(8,128)(2,1)S(1)}, u32[]{:S(2)}, u32[]{:S(2)}) collective-permute-start(bf16[288,128]{1,0:T(8,128)(2,1)S(1)} %get-tuple-element.12), channel_id=1, source_target_pairs={{0,1},{1,0},{2,3},{3,2},{4,5},{5,4},{6,7},{7,6},{8,9},{9,8},{10,11... | collective-permute-start | bytes 221192 | tf_op jit(solution)/shard_map/ppermute | solution.py:405
  28.6 1.5 %collective-permute-start.1 = (bf16[288,128]{1,0:T(8,128)(2,1)S(1)}, bf16[288,128]{1,0:T(8,128)(2,1)S(1)}, u32[]{:S(2)}, u32[]{:S(2)}) collective-permute-start(bf16[288,128]{1,0:T(8,128)(2,1)S(1)} %get-tuple-element.12), channel_id=1, source_target_pairs={{0,2},{1,3},{2,0},{3,1},{4,6},{5,7},{6,4},{7,5},{8,10},{9,11},{10,... | collective-permute-start | bytes 221192 | tf_op jit(solution)/shard_map/ppermute | solution.py:405
  30.1 0.5 collective-permute-start.2
  30.6 0.9 %collective-permute-done = bf16[288,128]{1,0:T(8,128)(2,1)S(1)} collective-permute-done((bf16[288,128]{1,0:T(8,128)(2,1)S(1)}, bf16[288,128]{1,0:T(8,128)(2,1)S(1)}, u32[]{:S(2)}, u32[]{:S(2)}) %collective-permute-start) | collective-permute-done | bytes 73760 | tf_op jit(solution)/shard_map/ppermute | solution.py:405
  31.5 2.3 %collective-permute-done.1 = bf16[288,128]{1,0:T(8,128)(2,1)S(1)} collective-permute-done((bf16[288,128]{1,0:T(8,128)(2,1)S(1)}, bf16[288,128]{1,0:T(8,128)(2,1)S(1)}, u32[]{:S(2)}, u32[]{:S(2)}) %collective-permute-start.1) | collective-permute-done | bytes 73760 | tf_op jit(solution)/shard_map/ppermute | solution.py:405
  33.8 1.6 %collective-permute-done.2 = bf16[288,128]{1,0:T(8,128)(2,1)S(1)} collective-permute-done((bf16[288,128]{1,0:T(8,128)(2,1)S(1)}, bf16[288,128]{1,0:T(8,128)(2,1)S(1)}, u32[]{:S(2)}, u32[]{:S(2)}) %collective-permute-start.2) | collective-permute-done | bytes 73760 | tf_op jit(solution)/shard_map/ppermute | solution.py:405
  35.4 0.7 %fusion.2.product_ref = f32[16,128]{1,0:T(8,128)S(1)} fusion(bf16[128,72,128]{2,1,0:T(8,128)(2,1)S(1)} %get-tuple-element.13, bf16[16,72,128]{2,1,0:T(8,128)(2,1)S(1)} %bitcast.18), kind=kOutput, calls=%fused_computation.2 | convolution fusion | flops 37748736 | bytes 2662400 | tf_op jit(solution)/shard_map/dot_general | solution.py:408
  36.1 0.7 %share.1 = f32[8,24,128]{2,1,0:T(8,128)} custom-call(f32[16,128]{1,0:T(8,128)S(1)} %fusion.2.product_ref, f32[2,128]{1,0:T(2,128)S(1)} %get-tuple-element.14.sums_ref), custom_call_target="tpu_custom_call" | custom-call | tf_op jit(solution)/shard_map/share/pallas_call | solution.py:100
  36.8 3.4 %all-to-all-start.2 = ((f32[8,24,128]{2,1,0:T(8,128)}), f32[8,24,128]{2,1,0:T(8,128)S(1)}, u32[]{:S(2)}, u32[]{:S(2)}) async-start(f32[8,24,128]{2,1,0:T(8,128)} %share.1), calls=%async_computation.2 | async-start | bytes 196608 | tf_op jit(solution)/shard_map/all_to_all | solution.py:415
  40.2 6.2 %all-to-all-done.2.copies_ref = f32[8,24,128]{2,1,0:T(8,128)S(1)} async-done(((f32[8,24,128]{2,1,0:T(8,128)}), f32[8,24,128]{2,1,0:T(8,128)S(1)}, u32[]{:S(2)}, u32[]{:S(2)}) %all-to-all-start.2) | async-done | bytes 98336 | tf_op jit(solution)/shard_map/all_to_all | solution.py:415
  46.4 0.0 copy-done.2
  46.4 0.9 %finish.1 = (f32[144,128]{1,0:T(8,128)}, f32[2,4,64]{2,1,0:T(4,128)}, f32[2,4,64]{2,1,0:T(4,128)}) custom-call(s32[1]{0:T(128)} %bitcast.band_ref, f32[128,128]{1,0:T(8,128)S(1)} %copy-done.2, f32[8,24,128]{2,1,0:T(8,128)S(1)} %all-to-all-done.2.copies_ref, f32[144,128]{1,0:T(8,128)S(1)} %get-tuple-element.15.image_ref, f32[144,128]{1,0:T(8,128)S(1)} %bitcast.13), custom_call_target="tpu_custom_call" | custom-call | tf_op jit(solution)/shard_map/finish/pallas_call | solution.py:378
  (1 shorter events, 0.0 us)
Async XLA Ops:
  0.6 26.2 %copy-start = (f32[1,2,72,128]{3,2,1,0:T(8,128)S(1)}, f32[1,2,72,128]{3,2,1,0:T(8,128)}, u32[]{:S(2)}) copy-start(f32[1,2,72,128]{3,2,1,0:T(8,128)} %param.12) | copy-start | bytes 221188
  0.6 26.2 %copy-start.1 = (bf16[432,256]{1,0:T(8,128)(2,1)S(1)}, bf16[432,256]{1,0:T(8,128)(2,1)}, u32[]{:S(2)}) copy-start(bf16[432,256]{1,0:T(8,128)(2,1)} %constant.24.clone.table_ref) | copy-start | bytes 663556
  0.7 26.2 %copy-start.3 = (s32[128]{0:T(128)S(1)}, s32[128]{0:T(128)}, u32[]{:S(2)}) copy-start(s32[128]{0:T(128)} %param.14) | copy-start | bytes 1540
  18.4 28.0 %copy-start.2 = (f32[128,128]{1,0:T(8,128)S(1)}, f32[128,128]{1,0:T(8,128)}, u32[]{:S(2)}) copy-start(f32[128,128]{1,0:T(8,128)} %constant.25.clone.table_ref) | copy-start | bytes 196612
  27.0 4.4 %collective-permute-start = (bf16[288,128]{1,0:T(8,128)(2,1)S(1)}, bf16[288,128]{1,0:T(8,128)(2,1)S(1)}, u32[]{:S(2)}, u32[]{:S(2)}) collective-permute-start(bf16[288,128]{1,0:T(8,128)(2,1)S(1)} %get-tuple-element.12), channel_id=1, source_target_pairs={{0,1},{1,0},{2,3},{3,2},{4,5},{5,4},{6,7},{7,6},{8,9},{9,8},{10,11... | collective-permute-start | bytes 221192 | tf_op jit(solution)/shard_map/ppermute | solution.py:405
  28.6 5.1 %collective-permute-start.1 = (bf16[288,128]{1,0:T(8,128)(2,1)S(1)}, bf16[288,128]{1,0:T(8,128)(2,1)S(1)}, u32[]{:S(2)}, u32[]{:S(2)}) collective-permute-start(bf16[288,128]{1,0:T(8,128)(2,1)S(1)} %get-tuple-element.12), channel_id=1, source_target_pairs={{0,2},{1,3},{2,0},{3,1},{4,6},{5,7},{6,4},{7,5},{8,10},{9,11},{10,... | collective-permute-start | bytes 221192 | tf_op jit(solution)/shard_map/ppermute | solution.py:405
  30.1 5.3 %collective-permute-start.2 = (bf16[288,128]{1,0:T(8,128)(2,1)S(1)}, bf16[288,128]{1,0:T(8,128)(2,1)S(1)}, u32[]{:S(2)}, u32[]{:S(2)}) collective-permute-start(bf16[288,128]{1,0:T(8,128)(2,1)S(1)} %get-tuple-element.12), channel_id=1, source_target_pairs={{0,3},{1,2},{2,1},{3,0},{4,7},{5,6},{6,5},{7,4},{8,11},{9,10},{10,... | collective-permute-start | bytes 221192 | tf_op jit(solution)/shard_map/ppermute | solution.py:405
  36.8 9.6 %all-to-all-start.2 = ((f32[8,24,128]{2,1,0:T(8,128)}), f32[8,24,128]{2,1,0:T(8,128)S(1)}, u32[]{:S(2)}, u32[]{:S(2)}) async-start(f32[8,24,128]{2,1,0:T(8,128)} %share.1), calls=%async_computation.2 | async-start | bytes 196608 | tf_op jit(solution)/shard_map/all_to_all | solution.py:415

commit v3 on v2

--- a/solution.py
+++ b/solution.py
@@ -107,16 +107,22 @@
     )(*[pltpu.with_memory_space_constraint(operand, pltpu.VMEM) for operand in operands], *far)
 
 
-def spread_sticks(sizes, vector, positions):
+def spread_sticks(sizes, vector, positions, y_back):
     block = 2 * sizes.rows
-    far = (jnp.asarray(z_back_table(sizes)), vector, positions[None, :])
-
-    def kernel(table_far, vector_far, position_far, out_ref, table_ref, vector_ref, position_ref, sems):
-        pairs = ((vector_far, vector_ref), (table_far, table_ref), (position_far, position_ref))
-        copies = [pltpu.make_async_copy(far, near, sems.at[index]) for index, (far, near) in enumerate(pairs)]
+    z_table = jnp.asarray(z_back_table(sizes))
+    kept = (vector, positions[None, :], y_back)
+    far = (kept[0], z_table, *kept[1:])
+
+    def kernel(*refs):
+        distant, (out_ref, *near), (table_ref, sems) = refs[: len(far)], refs[len(far) : -2], refs[-2:]
+        vector_ref, position_ref = near[:2]
+        copies = [
+            pltpu.make_async_copy(source, target, sems.at[index])
+            for index, (source, target) in enumerate(zip(distant, (near[0], table_ref, *near[1:]), strict=True))
+        ]
         for copy in copies:
             copy.start()
-        for copy in copies:
+        for copy in copies[:3]:
             copy.wait()
         vector = vector_ref[...]
         high = vector.astype(bf16)
@@ -130,15 +136,17 @@
         for group in range(sizes.groups):
             out_ref[group, 0:block, :] = columns[group * block : (group + 1) * block].astype(bf16)
             out_ref[group, block:, :] = tail
+        for copy in copies[3:]:
+            copy.wait()
 
     return call_on_chip(
         kernel,
         "spread_sticks",
         (),
-        (((sizes.groups, block + 16, sizes.sticks_local), bf16),),
+        (((sizes.groups, block + 16, sizes.sticks_local), bf16), *[(array.shape, array.dtype) for array in kept]),
         far,
-        [pltpu.VMEM(operand.shape, operand.dtype) for operand in far] + [pltpu.SemaphoreType.DMA((3,))],
-    )[0]
+        [pltpu.VMEM(z_table.shape, z_table.dtype), pltpu.SemaphoreType.DMA((len(far),))],
+    )
 
 
 def turn(position, size):
@@ -181,23 +189,30 @@
     return results
 
 
-def apply_planes(sizes, received, potential, psi_res):
-    far = (*[jnp.asarray(t) for t in plane_tables(sizes)], potential, psi_res)
+def apply_planes(sizes, received, near, later, psi_res):
     grid, box, line, rows = sizes.grid, sizes.box, sizes.line, sizes.rows
     groups, local, sticks = sizes.groups, sizes.sticks_local, sizes.sticks
     low_count, high_count = sizes.low_count, sizes.high_count
     columns = low_count * line
     half = high_count * rows
 
-    def kernel(in_ref, *refs):
-        distant, (out_ref, psi_ref), near = refs[:6], refs[6:8], refs[8:13]
-        left_ref, hot_ref, a_ref, b_ref, sems = refs[13:]
-        yb_ref, xb_ref, xf_ref, yf_ref, pot_ref = near
+    psi_bytes, other_bytes = (sum(array.nbytes for array in arrays) for arrays in ((psi_res,), (received, received, near)))
+    bring = psi_bytes + other_bytes < 3200000
+
+    def kernel(in_ref, yb_ref, *refs):
+        *distant, out_ref = refs[:5]
+        scratch = refs[5:]
+        if bring:
+            *distant, psi_far = refs[:5]
+            out_ref, psi_ref, *scratch = refs[5:]
+        *near_refs, left_ref, hot_ref, a_ref, b_ref, sems = scratch
+        xb_ref, pot_ref, xf_ref, yf_ref = near_refs
         copies = [
             pltpu.make_async_copy(source, target, sems.at[index])
-            for index, (source, target) in enumerate(zip(distant, (*near, psi_ref), strict=True))
+            for index, (source, target) in enumerate(zip(distant, near_refs, strict=True))
         ]
-        yb_copy, xb_copy, xf_copy, yf_copy, pot_copy, psi_copy = copies
+        if bring:
+            copies.append(pltpu.make_async_copy(psi_far, psi_ref, sems.at[4]))
         for copy in copies:
             copy.start()
 
@@ -230,7 +245,6 @@
                     )
 
         placed = lax.dot_general(left_ref[...], hot_ref[...], (((1,), (1,)), ((), ())), preferred_element_type=f32)
-        yb_copy.wait()
         placed = jnp.concatenate(cross(placed[:half], placed[half:], line), 0).astype(bf16)
         lines = jnp.dot(jnp.concatenate([placed, placed], 1), yb_ref[...], preferred_element_type=f32)
         for part in range(2):
@@ -256,7 +270,7 @@
                         part * box : (part + 1) * box, index * grid : (index + 1) * grid
                     ]
 
-        for copy in (xb_copy, pot_copy, xf_copy):
+        for copy in copies[:3]:
             copy.wait()
         fields = [to_field(0)]
         for first in range(0, rows, 2):
@@ -264,7 +278,7 @@
                 fields.append(to_field(first + 2))
             from_field(first, fields[first // 2])
 
-        yf_copy.wait()
+        copies[3].wait()
         lines = jnp.concatenate([b_ref[0], b_ref[1]], 1).astype(bf16)
         boxed = jnp.dot(lines, yf_ref[...], preferred_element_type=f32)
         boxed = boxed[:, : 2 * line] + boxed[:, 2 * line :]
@@ -290,23 +304,26 @@
                         piece = found[start : start + rows, (g - first) * local : (g - first + 1) * local]
                         total = total + jnp.where(highs[g] == float(high), piece, 0.0)
                     out_ref[g, part * rows : (part + 1) * rows, :] = total.astype(bf16)
-        psi_copy.wait()
-
-    return call_on_chip(
+        for copy in copies[4:]:
+            copy.wait()
+
+    extra = (psi_res,) if bring else ()
+    picked, *brought = call_on_chip(
         kernel,
         "apply_planes",
-        (received,),
-        (((groups, 2 * rows, local), bf16), (psi_res.shape, psi_res.dtype)),
-        far,
+        (received, near),
+        (((groups, 2 * rows, local), bf16), *[(array.shape, array.dtype) for array in extra]),
+        (*later, *extra),
         (
-            *[pltpu.VMEM(operand.shape, operand.dtype) for operand in far[:5]],
+            *[pltpu.VMEM(array.shape, array.dtype) for array in later],
             pltpu.VMEM((2 * half, sticks), bf16),
             pltpu.VMEM((columns, sticks), bf16),
             pltpu.VMEM((2, box * rows, grid), f32),
             pltpu.VMEM((2, box * rows, grid), f32),
-            pltpu.SemaphoreType.DMA((6,)),
+            pltpu.SemaphoreType.DMA((5,)),
         ),
     )
+    return picked, brought[0] if bring else psi_res
 
 
 def image_sticks(sizes, columns, vector, positions):
@@ -332,7 +349,7 @@
     return call_on_chip(
         kernel,
         "image_sticks",
-        (jnp.asarray(z_forward_table(sizes)), columns, vector, positions[None, :]),
+        (jnp.asarray(z_forward_table(sizes)), columns, vector, positions),
         (((height, local), f32), ((2 * height, local), bf16), ((2, local), f32)),
     )
 
@@ -394,12 +411,14 @@
     potential = jnp.pad(local_potential, ((0, sizes.rows - planes), (0, 0), (0, 0)))
     vector = correction.reshape(2 * stick_depth, sticks_local)
 
-    moving = spread_sticks(sizes, vector, stick_xy)
+    y_back, x_back, x_forward, y_forward = [jnp.asarray(table) for table in plane_tables(sizes)]
+    moving, vector, positions, y_back = spread_sticks(sizes, vector, stick_xy, y_back)
+    later = (x_back, potential, x_forward, y_forward)
     moving = lax.all_to_all(moving, "pw", split_axis=0, concat_axis=0, tiled=True)
-    picked, psi_near = apply_planes(sizes, moving, potential, psi_res.reshape(2 * res_count, stick_depth, sticks_local))
+    picked, psi_near = apply_planes(sizes, moving, y_back, later, psi_res.reshape(2 * res_count, stick_depth, sticks_local))
     picked = lax.all_to_all(picked, "pw", split_axis=0, concat_axis=0, tiled=True)
     picked = picked.reshape(2 * sizes.rows * groups, sticks_local)
-    image, rounded, sums = image_sticks(sizes, picked, vector, stick_xy)
+    image, rounded, sums = image_sticks(sizes, picked, vector, positions)
 
     blocks = [rounded] + [
         lax.ppermute(rounded, "band", [(i, i ^ step) for i in range(band_total)]) for step in range(1, band_total)
@@ -411,9 +430,10 @@
         (((1, 2), (1, 2)), ((), ())),
         preferred_element_type=f32,
     )
+    band = lax.axis_index("band")[None]
+    product, band = lax.optimization_barrier((product, band))
     copies = share(product, sums, groups)
     copies = lax.all_to_all(copies, "pw", split_axis=0, concat_axis=0, tiled=True)
-    band = lax.axis_index("band")[None]
     residual, hamiltonian, intersection = finish(copies, image, vector, band, band_total, res_count)
     return (
         residual.reshape(correction.shape),

time: 47.6 us -> 45.1 us (0.947)
  blocking collectives: 20.9 us -> 29.6 us
  waiting for transfers between devices: 11 us -> 3.81 us
  starting transfers between devices: 6.91 us -> 3.55 us
  Pallas kernels: 6.98 us -> 6.4 us
    all_to_all x0 -> x1, blocking collectives: none -> 8.7 us  [shards(): lax.all_to_all(copies, 'pw', split_axis=0, concat_axis=0, tiled=True)]
    all_to_all x1 -> x0, waiting for transfers between devices: 6.24 us -> none  [shards(): lax.all_to_all(copies, 'pw', split_axis=0, concat_axis=0, tiled=True)]
    all_to_all x1 -> x0, starting transfers between devices: 3.36 us -> none  [shards(): lax.all_to_all(copies, 'pw', split_axis=0, concat_axis=0, tiled=True)]
    ppermute x3, waiting for transfers between devices: 4.78 us -> 3.81 us  [shards(): lax.ppermute(rounded, 'band', [(i, i ^ step) for i in range(band_total)])]
    pallas_call x4, Pallas kernels: 6.12 us -> 5.55 us  [call_on_chip(): pl.pallas_call(kernel, out_shape=tuple((pltpu.VMEM(shape, dtype) for shap...]
  transfers between devices with their start and end apart: 4 -> 3, of which waited for: 4 -> 3; matrix products, arithmetic and copies ran while one was open for 0% -> 0% of each run, Pallas kernels for 0% -> 0%
where the time goes in v3:
time: 45.1 us; the launch traced here: 44.8 us
  blocking collectives  29.6 us (66%)
  Pallas kernels  6.4 us (14%)
  waiting for transfers between devices  3.81 us (8%)
  starting transfers between devices  3.55 us (8%)
  matrix products  0.7 us (2%)
  between operations  0.68 us (2%)
    all_to_all x1, blocking collectives, shards(): lax.all_to_all(moving, 'pw', split_axis=0, concat_axis=0, tiled=True)  12.5 us
    all_to_all x1, blocking collectives, shards(): lax.all_to_all(copies, 'pw', split_axis=0, concat_axis=0, tiled=True)  8.7 us
    all_to_all x1, blocking collectives, shards(): lax.all_to_all(picked, 'pw', split_axis=0, concat_axis=0, tiled=True)  8.43 us
    pallas_call x4, Pallas kernels, call_on_chip(): pl.pallas_call(kernel, out_shape=tuple((pltpu.VMEM(shape, dtype) for shap...  5.55 us
    ppermute x3, waiting for transfers between devices, shards(): lax.ppermute(rounded, 'band', [(i, i ^ step) for i in range(band_total)])  3.81 us
    ppermute x3, starting transfers between devices, shards(): lax.ppermute(rounded, 'band', [(i, i ^ step) for i in range(band_total)])  3.55 us
  transfers between devices with their start and end apart: 3, of which 3 were waited for; matrix products, arithmetic and copies ran while one was open for 0% of the time, Pallas kernels for 0%

profile of v3, /device:TPU:0, one launch (start us, length us, event | category | flops | bytes accessed | tf_op | source)
XLA Modules:
  0.0 44.8 jit_solution(1956924517138831856)
XLA Ops:
  0.6 0.0 copy-start
  0.6 1.3 %spread_sticks.1 = (bf16[8,48,128]{2,1,0:T(8,128)(2,1)S(1)}, f32[144,128]{1,0:T(8,128)S(1)}, s32[1,128]{1,0:T(1,128)S(1)}, bf16[256,256]{1,0:T(8,128)(2,1)S(1)}) custom-call(f32[144,128]{1,0:T(8,128)} %bitcast.14, bf16[256,432]{1,0:T(8,128)(2,1)} %constant.23.clone.refs_1_, s32[1,128]{1,0:T(1,128)} %bitcast.15, bf16[256,256]{1,0:T(8,128)(2,1)} %constant.9.clone.refs_3_), custom_call_target="tpu_custom_call" | custom-call | tf_op jit(solution)/shard_map/spread_sticks/pallas_call | solution.py:100
  1.9 12.5 %all_to_all.15.in_ref = bf16[8,48,128]{2,1,0:T(8,128)(2,1)S(1)} all-to-all(bf16[8,48,128]{2,1,0:T(8,128)(2,1)S(1)} %get-tuple-element.17), channel_id=1, replica_groups=mesh['pw'=8,'band'=4] {'pw'}, dimensions={0} | all-to-all | bytes 196608 | tf_op jit(solution)/shard_map/all_to_all | solution.py:417
  14.4 4.0 %apply_planes.1 = (bf16[8,32,128]{2,1,0:T(8,128)(2,1)S(1)}, bf16[128,72,128]{2,1,0:T(8,128)(2,1)S(1)}) custom-call(bf16[8,48,128]{2,1,0:T(8,128)(2,1)S(1)} %all_to_all.15.in_ref, bf16[256,256]{1,0:T(8,128)(2,1)S(1)} %get-tuple-element.18.yb_ref, bf16[256,240]{1,0:T(8,128)(2,1)} %constant.20.clone.refs_0_, f32[16,128,128]{2,1,0:T(8,128)} %refs_1_.2, ...), custom_call_target="tpu_custom_call" | custom-call | tf_op jit(solution)/shard_map/apply_planes/pallas_call | solution.py:100
  18.4 0.0 copy-start.1
  18.4 8.4 %all_to_all.16 = bf16[8,32,128]{2,1,0:T(8,128)(2,1)S(1)} all-to-all(bf16[8,32,128]{2,1,0:T(8,128)(2,1)S(1)} %get-tuple-element.19), channel_id=1, replica_groups=mesh['pw'=8,'band'=4] {'pw'}, dimensions={0} | all-to-all | bytes 131072 | tf_op jit(solution)/shard_map/all_to_all | solution.py:419
  26.8 0.0 copy-done
  26.8 0.2 image_sticks.1
  27.1 2.5 %collective-permute-start.2 = (bf16[288,128]{1,0:T(8,128)(2,1)S(1)}, bf16[288,128]{1,0:T(8,128)(2,1)S(1)}, u32[]{:S(2)}, u32[]{:S(2)}) collective-permute-start(bf16[288,128]{1,0:T(8,128)(2,1)S(1)} %get-tuple-element.22), channel_id=1, source_target_pairs={{0,3},{1,2},{2,1},{3,0},{4,7},{5,6},{6,5},{7,4},{8,11},{9,10},{10,... | collective-permute-start | bytes 221192 | tf_op jit(solution)/shard_map/ppermute | solution.py:424
  29.6 0.5 %collective-permute-start.1 = (bf16[288,128]{1,0:T(8,128)(2,1)S(1)}, bf16[288,128]{1,0:T(8,128)(2,1)S(1)}, u32[]{:S(2)}, u32[]{:S(2)}) collective-permute-start(bf16[288,128]{1,0:T(8,128)(2,1)S(1)} %get-tuple-element.22), channel_id=1, source_target_pairs={{0,2},{1,3},{2,0},{3,1},{4,6},{5,7},{6,4},{7,5},{8,10},{9,11},{10,... | collective-permute-start | bytes 221192 | tf_op jit(solution)/shard_map/ppermute | solution.py:424
  30.1 0.5 %collective-permute-start = (bf16[288,128]{1,0:T(8,128)(2,1)S(1)}, bf16[288,128]{1,0:T(8,128)(2,1)S(1)}, u32[]{:S(2)}, u32[]{:S(2)}) collective-permute-start(bf16[288,128]{1,0:T(8,128)(2,1)S(1)} %get-tuple-element.22), channel_id=1, source_target_pairs={{0,1},{1,0},{2,3},{3,2},{4,5},{5,4},{6,7},{7,6},{8,9},{9,8},{10,11... | collective-permute-start | bytes 221192 | tf_op jit(solution)/shard_map/ppermute | solution.py:424
  30.6 1.9 %collective-permute-done.2 = bf16[288,128]{1,0:T(8,128)(2,1)S(1)} collective-permute-done((bf16[288,128]{1,0:T(8,128)(2,1)S(1)}, bf16[288,128]{1,0:T(8,128)(2,1)S(1)}, u32[]{:S(2)}, u32[]{:S(2)}) %collective-permute-start.2) | collective-permute-done | bytes 73760 | tf_op jit(solution)/shard_map/ppermute | solution.py:424
  32.5 1.4 %collective-permute-done.1 = bf16[288,128]{1,0:T(8,128)(2,1)S(1)} collective-permute-done((bf16[288,128]{1,0:T(8,128)(2,1)S(1)}, bf16[288,128]{1,0:T(8,128)(2,1)S(1)}, u32[]{:S(2)}, u32[]{:S(2)}) %collective-permute-start.1) | collective-permute-done | bytes 73760 | tf_op jit(solution)/shard_map/ppermute | solution.py:424
  33.9 0.5 %collective-permute-done = bf16[288,128]{1,0:T(8,128)(2,1)S(1)} collective-permute-done((bf16[288,128]{1,0:T(8,128)(2,1)S(1)}, bf16[288,128]{1,0:T(8,128)(2,1)S(1)}, u32[]{:S(2)}, u32[]{:S(2)}) %collective-permute-start) | collective-permute-done | bytes 73760 | tf_op jit(solution)/shard_map/ppermute | solution.py:424
  34.5 0.7 %fusion.2.product_ref = f32[16,128]{1,0:T(8,128)S(1)} fusion(bf16[128,72,128]{2,1,0:T(8,128)(2,1)S(1)} %get-tuple-element.23, bf16[16,72,128]{2,1,0:T(8,128)(2,1)S(1)} %bitcast.13), kind=kOutput, calls=%fused_computation.2 | convolution fusion | flops 37748736 | bytes 2662400 | tf_op jit(solution)/shard_map/dot_general | solution.py:427
  35.2 8.7 %all_to_all.17.copies_ref = f32[8,24,128]{2,1,0:T(8,128)S(1)} all-to-all(f32[8,24,128]{2,1,0:T(8,128)S(1)} %share.1), channel_id=1, replica_groups=mesh['pw'=8,'band'=4] {'pw'}, dimensions={0} | all-to-all | bytes 196608 | tf_op jit(solution)/shard_map/all_to_all | solution.py:436
  43.9 0.0 copy-done.1
  43.9 0.9 %finish.1 = (f32[144,128]{1,0:T(8,128)}, f32[2,4,64]{2,1,0:T(4,128)}, f32[2,4,64]{2,1,0:T(4,128)}) custom-call(s32[1]{0:T(128)} %bitcast.6.band_ref, f32[128,128]{1,0:T(8,128)S(1)} %copy-done.1, f32[8,24,128]{2,1,0:T(8,128)S(1)} %all_to_all.17.copies_ref, f32[144,128]{1,0:T(8,128)S(1)} %get-tuple-element.27.image_ref, ...), custom_call_target="tpu_custom_call" | custom-call | tf_op jit(solution)/shard_map/finish/pallas_call | solution.py:395
  (2 shorter events, 0.0 us)
Async XLA Ops:
  0.6 26.2 %copy-start = (bf16[432,256]{1,0:T(8,128)(2,1)S(1)}, bf16[432,256]{1,0:T(8,128)(2,1)}, u32[]{:S(2)}) copy-start(bf16[432,256]{1,0:T(8,128)(2,1)} %constant.24.clone.table_ref) | copy-start | bytes 663556
  18.4 25.5 %copy-start.1 = (f32[128,128]{1,0:T(8,128)S(1)}, f32[128,128]{1,0:T(8,128)}, u32[]{:S(2)}) copy-start(f32[128,128]{1,0:T(8,128)} %constant.25.clone.table_ref) | copy-start | bytes 196612
  27.1 5.4 %collective-permute-start.2 = (bf16[288,128]{1,0:T(8,128)(2,1)S(1)}, bf16[288,128]{1,0:T(8,128)(2,1)S(1)}, u32[]{:S(2)}, u32[]{:S(2)}) collective-permute-start(bf16[288,128]{1,0:T(8,128)(2,1)S(1)} %get-tuple-element.22), channel_id=1, source_target_pairs={{0,3},{1,2},{2,1},{3,0},{4,7},{5,6},{6,5},{7,4},{8,11},{9,10},{10,... | collective-permute-start | bytes 221192 | tf_op jit(solution)/shard_map/ppermute | solution.py:424
  29.6 4.4 %collective-permute-start.1 = (bf16[288,128]{1,0:T(8,128)(2,1)S(1)}, bf16[288,128]{1,0:T(8,128)(2,1)S(1)}, u32[]{:S(2)}, u32[]{:S(2)}) collective-permute-start(bf16[288,128]{1,0:T(8,128)(2,1)S(1)} %get-tuple-element.22), channel_id=1, source_target_pairs={{0,2},{1,3},{2,0},{3,1},{4,6},{5,7},{6,4},{7,5},{8,10},{9,11},{10,... | collective-permute-start | bytes 221192 | tf_op jit(solution)/shard_map/ppermute | solution.py:424
  30.1 4.4 %collective-permute-start = (bf16[288,128]{1,0:T(8,128)(2,1)S(1)}, bf16[288,128]{1,0:T(8,128)(2,1)S(1)}, u32[]{:S(2)}, u32[]{:S(2)}) collective-permute-start(bf16[288,128]{1,0:T(8,128)(2,1)S(1)} %get-tuple-element.22), channel_id=1, source_target_pairs={{0,1},{1,0},{2,3},{3,2},{4,5},{5,4},{6,7},{7,6},{8,9},{9,8},{10,11... | collective-permute-start | bytes 221192 | tf_op jit(solution)/shard_map/ppermute | solution.py:424

commit v4 on v3

--- a/solution.py
+++ b/solution.py
@@ -72,7 +72,7 @@
     table = phases(z_freq, z_index, -1, sizes.grid) * real / float(sizes.grid**3)
     table = table.reshape(2 * sizes.depth, 2, sizes.groups, sizes.rows)
     table = table.transpose(0, 2, 1, 3).reshape(2 * sizes.depth, -1)
-    return np.concatenate(split(table, 3), 0)
+    return np.concatenate(split(table, 2), 0)
 
 
 def plane_tables(sizes):
@@ -107,10 +107,10 @@
     )(*[pltpu.with_memory_space_constraint(operand, pltpu.VMEM) for operand in operands], *far)
 
 
-def spread_sticks(sizes, vector, positions, y_back):
+def spread_sticks(sizes, vector, positions, others):
     block = 2 * sizes.rows
     z_table = jnp.asarray(z_back_table(sizes))
-    kept = (vector, positions[None, :], y_back)
+    kept = (vector, positions[None, :], *others)
     far = (kept[0], z_table, *kept[1:])
 
     def kernel(*refs):
@@ -189,33 +189,14 @@
     return results
 
 
-def apply_planes(sizes, received, near, later, psi_res):
+def apply_planes(sizes, received, near):
     grid, box, line, rows = sizes.grid, sizes.box, sizes.line, sizes.rows
     groups, local, sticks = sizes.groups, sizes.sticks_local, sizes.sticks
     low_count, high_count = sizes.low_count, sizes.high_count
     columns = low_count * line
     half = high_count * rows
 
-    psi_bytes, other_bytes = (sum(array.nbytes for array in arrays) for arrays in ((psi_res,), (received, received, near)))
-    bring = psi_bytes + other_bytes < 3200000
-
-    def kernel(in_ref, yb_ref, *refs):
-        *distant, out_ref = refs[:5]
-        scratch = refs[5:]
-        if bring:
-            *distant, psi_far = refs[:5]
-            out_ref, psi_ref, *scratch = refs[5:]
-        *near_refs, left_ref, hot_ref, a_ref, b_ref, sems = scratch
-        xb_ref, pot_ref, xf_ref, yf_ref = near_refs
-        copies = [
-            pltpu.make_async_copy(source, target, sems.at[index])
-            for index, (source, target) in enumerate(zip(distant, near_refs, strict=True))
-        ]
-        if bring:
-            copies.append(pltpu.make_async_copy(psi_far, psi_ref, sems.at[4]))
-        for copy in copies:
-            copy.start()
-
+    def kernel(in_ref, yb_ref, xb_ref, xf_ref, yf_ref, pot_ref, out_ref, left_ref, hot_ref, a_ref, b_ref):
         def relative(row):
             position = jnp.concatenate([in_ref[g, 2 * rows : 2 * rows + 16, :].astype(f32)[row : row + 1] for g in range(groups)], 0)
             moved = position - anchor_of(position, grid) + float(box // 2)
@@ -270,15 +251,12 @@
                         part * box : (part + 1) * box, index * grid : (index + 1) * grid
                     ]
 
-        for copy in copies[:3]:
-            copy.wait()
         fields = [to_field(0)]
         for first in range(0, rows, 2):
             if first + 2 < rows:
                 fields.append(to_field(first + 2))
             from_field(first, fields[first // 2])
 
-        copies[3].wait()
         lines = jnp.concatenate([b_ref[0], b_ref[1]], 1).astype(bf16)
         boxed = jnp.dot(lines, yf_ref[...], preferred_element_type=f32)
         boxed = boxed[:, : 2 * line] + boxed[:, 2 * line :]
@@ -304,26 +282,19 @@
                         piece = found[start : start + rows, (g - first) * local : (g - first + 1) * local]
                         total = total + jnp.where(highs[g] == float(high), piece, 0.0)
                     out_ref[g, part * rows : (part + 1) * rows, :] = total.astype(bf16)
-        for copy in copies[4:]:
-            copy.wait()
-
-    extra = (psi_res,) if bring else ()
-    picked, *brought = call_on_chip(
+
+    return call_on_chip(
         kernel,
         "apply_planes",
-        (received, near),
-        (((groups, 2 * rows, local), bf16), *[(array.shape, array.dtype) for array in extra]),
-        (*later, *extra),
-        (
-            *[pltpu.VMEM(array.shape, array.dtype) for array in later],
+        (received, *near),
+        (((groups, 2 * rows, local), bf16),),
+        scratch=(
             pltpu.VMEM((2 * half, sticks), bf16),
             pltpu.VMEM((columns, sticks), bf16),
             pltpu.VMEM((2, box * rows, grid), f32),
             pltpu.VMEM((2, box * rows, grid), f32),
-            pltpu.SemaphoreType.DMA((5,)),
         ),
-    )
-    return picked, brought[0] if bring else psi_res
+    )[0]
 
 
 def image_sticks(sizes, columns, vector, positions):
@@ -332,7 +303,7 @@
 
     def kernel(table_ref, columns_ref, vector_ref, position_ref, image_ref, rounded_ref, sums_ref):
         product = jnp.dot(table_ref[...], columns_ref[...], preferred_element_type=f32)
-        applied = product[:height] + (product[height : 2 * height] + product[2 * height :])
+        applied = product[:height] + product[height:]
         vector = vector_ref[...]
         x_freq = signed_freq(position_ref[...] // grid, grid)
         y_freq = signed_freq(position_ref[...] % grid, grid)
@@ -354,6 +325,17 @@
     )
 
 
+def bring(array, after):
+    def kernel(after_ref, far_ref, out_ref, sem):
+        copy = pltpu.make_async_copy(far_ref, out_ref, sem)
+        copy.start()
+        copy.wait()
+
+    return call_on_chip(
+        kernel, "bring", (after,), ((array.shape, array.dtype),), (array,), (pltpu.SemaphoreType.DMA(()),)
+    )[0]
+
+
 def share(product, sums, groups):
     count, width = product.shape
     height = round_up(count + 2, 8)
@@ -370,17 +352,17 @@
 def finish(copies, image, vector, band, band_total, res_count):
     count = copies.shape[0]
     width = 2 * res_count
-    table = np.zeros((width, width), np.float32)
-    lane = np.arange(width)
-    table[lane, lane % 2 * res_count + lane // 2] = 1.0
-
-    def kernel(band_ref, table_ref, copies_ref, image_ref, vector_ref, residual_ref, ham_ref, inter_ref, total_ref):
+
+    def kernel(band_ref, copies_ref, image_ref, vector_ref, residual_ref, ham_ref, inter_ref, total_ref):
         total = copies_ref[0]
         for index in range(1, count):
             total = total + copies_ref[index]
         tail = jnp.sum(total[4 * band_total : 4 * band_total + 2], axis=1, keepdims=True)
         residual_ref[...] = image_ref[...] - (tail[0:1] / tail[1:2]) * vector_ref[...]
-        total_ref[...] = jnp.dot(total[: 4 * band_total], table_ref[...], precision=highest, preferred_element_type=f32)
+        source = lax.broadcasted_iota(jnp.int32, (width, width), 0)
+        target = lax.broadcasted_iota(jnp.int32, (width, width), 1)
+        table = jnp.where(target == source % 2 * res_count + source // 2, 1.0, 0.0)
+        total_ref[...] = jnp.dot(total[: 4 * band_total], table, precision=highest, preferred_element_type=f32)
         for column in range(band_total):
             source = column ^ band_ref[0]
             for index, out_ref in enumerate((inter_ref, ham_ref)):
@@ -390,12 +372,12 @@
                 out_ref[1, column : column + 1, :] = imag[:, :res_count] - real[:, res_count:]
 
     spec = pl.BlockSpec(memory_space=pltpu.VMEM)
-    operands = (jnp.asarray(table), copies, image, vector)
+    operands = (copies, image, vector)
     projection = jax.ShapeDtypeStruct((2, band_total, res_count), f32)
     return pl.pallas_call(
         kernel,
         out_shape=(jax.ShapeDtypeStruct(image.shape, f32), projection, projection),
-        in_specs=[pl.BlockSpec(memory_space=pltpu.SMEM)] + [spec] * 4,
+        in_specs=[pl.BlockSpec(memory_space=pltpu.SMEM)] + [spec] * 3,
         out_specs=(spec,) * 3,
         scratch_shapes=[pltpu.VMEM((4 * band_total, width), f32)],
         name="finish",
@@ -411,11 +393,10 @@
     potential = jnp.pad(local_potential, ((0, sizes.rows - planes), (0, 0), (0, 0)))
     vector = correction.reshape(2 * stick_depth, sticks_local)
 
-    y_back, x_back, x_forward, y_forward = [jnp.asarray(table) for table in plane_tables(sizes)]
-    moving, vector, positions, y_back = spread_sticks(sizes, vector, stick_xy, y_back)
-    later = (x_back, potential, x_forward, y_forward)
+    others = [*[jnp.asarray(table) for table in plane_tables(sizes)], potential]
+    moving, vector, positions, *near = spread_sticks(sizes, vector, stick_xy, others)
     moving = lax.all_to_all(moving, "pw", split_axis=0, concat_axis=0, tiled=True)
-    picked, psi_near = apply_planes(sizes, moving, y_back, later, psi_res.reshape(2 * res_count, stick_depth, sticks_local))
+    picked = apply_planes(sizes, moving, near)
     picked = lax.all_to_all(picked, "pw", split_axis=0, concat_axis=0, tiled=True)
     picked = picked.reshape(2 * sizes.rows * groups, sticks_local)
     image, rounded, sums = image_sticks(sizes, picked, vector, positions)
@@ -423,6 +404,7 @@
     blocks = [rounded] + [
         lax.ppermute(rounded, "band", [(i, i ^ step) for i in range(band_total)]) for step in range(1, band_total)
     ]
+    psi_near = bring(psi_res.reshape(2 * res_count, stick_depth, sticks_local), sums)
     joined = jnp.concatenate(blocks, 0).reshape(4 * band_total, stick_depth, sticks_local)
     product = lax.dot_general(
         joined,

time: 45.1 us -> 45.2 us (level)
  Pallas kernels: 6.4 us -> 7.43 us
  waiting for transfers between devices: 3.81 us -> 3.09 us
    pallas_call x4 -> x5, Pallas kernels: 5.55 us -> 6.57 us  [call_on_chip(): pl.pallas_call(kernel, out_shape=tuple((pltpu.VMEM(shape, dtype) for shap...]
    ppermute x3, waiting for transfers between devices: 3.81 us -> 3.09 us  [shards(): lax.ppermute(rounded, 'band', [(i, i ^ step) for i in range(band_total)])]
  transfers between devices with their start and end apart: 3 -> 3, of which waited for: 3 -> 2; matrix products, arithmetic and copies ran while one was open for 0% -> 0% of each run, Pallas kernels for 0% -> 4%
where the time goes in v4:
time: 45.2 us; the launch traced here: 44.9 us
  blocking collectives  29.5 us (65%)
  Pallas kernels  7.43 us (16%)
  starting transfers between devices  3.55 us (8%)
  waiting for transfers between devices  3.09 us (7%)
  matrix products  0.7 us (2%)
  between operations  0.69 us (2%)
    all_to_all x1, blocking collectives, shards(): lax.all_to_all(moving, 'pw', split_axis=0, concat_axis=0, tiled=True)  12.5 us
    all_to_all x1, blocking collectives, shards(): lax.all_to_all(copies, 'pw', split_axis=0, concat_axis=0, tiled=True)  8.7 us
    all_to_all x1, blocking collectives, shards(): lax.all_to_all(picked, 'pw', split_axis=0, concat_axis=0, tiled=True)  8.3 us
    pallas_call x5, Pallas kernels, call_on_chip(): pl.pallas_call(kernel, out_shape=tuple((pltpu.VMEM(shape, dtype) for shap...  6.57 us
    ppermute x3, starting transfers between devices, shards(): lax.ppermute(rounded, 'band', [(i, i ^ step) for i in range(band_total)])  3.55 us
    ppermute x3, waiting for transfers between devices, shards(): lax.ppermute(rounded, 'band', [(i, i ^ step) for i in range(band_total)])  3.09 us
  transfers between devices with their start and end apart: 3, of which 2 were waited for; matrix products, arithmetic and copies ran while one was open for 0% of the time, Pallas kernels for 4%

profile of v4, /device:TPU:0, one launch (start us, length us, event | category | flops | bytes accessed | tf_op | source)
XLA Modules:
  0.0 44.9 jit_solution(16500854027612277107)
XLA Ops:
  0.6 0.0 copy-start
  0.6 1.7 %spread_sticks.1 = (bf16[8,48,128]{2,1,0:T(8,128)(2,1)S(1)}, f32[144,128]{1,0:T(8,128)S(1)}, s32[1,128]{1,0:T(1,128)S(1)}, bf16[256,256]{1,0:T(8,128)(2,1)S(1)},...) custom-call(f32[144,128]{1,0:T(8,128)} %bitcast.14, ...), custom_call_target="tpu_custom_call" | custom-call | tf_op jit(solution)/shard_map/spread_sticks/pallas_call | solution.py:100
  2.3 12.5 %all_to_all.15.in_ref = bf16[8,48,128]{2,1,0:T(8,128)(2,1)S(1)} all-to-all(bf16[8,48,128]{2,1,0:T(8,128)(2,1)S(1)} %get-tuple-element.19), channel_id=1, replica_groups=mesh['pw'=8,'band'=4] {'pw'}, dimensions={0} | all-to-all | bytes 196608 | tf_op jit(solution)/shard_map/all_to_all | solution.py:398
  14.8 3.0 %apply_planes.1 = bf16[8,32,128]{2,1,0:T(8,128)(2,1)S(1)} custom-call(bf16[8,48,128]{2,1,0:T(8,128)(2,1)S(1)} %all_to_all.15.in_ref, bf16[256,256]{1,0:T(8,128)(2,1)S(1)} %get-tuple-element.20.yb_ref, bf16[256,240]{1,0:T(8,128)(2,1)S(1)} %get-tuple-element.21.xb_ref, bf16[160,256]{1,0:T(8,128)(2,1)S(1)} %get-tuple-element.22.xf_ref, ...), custom_call_target="tpu_custom_call" | custom-call | tf_op jit(solution)/shard_map/apply_planes/pallas_call | solution.py:100
  17.8 8.3 %all_to_all.16 = bf16[8,32,128]{2,1,0:T(8,128)(2,1)S(1)} all-to-all(bf16[8,32,128]{2,1,0:T(8,128)(2,1)S(1)} %apply_planes.1), channel_id=1, replica_groups=mesh['pw'=8,'band'=4] {'pw'}, dimensions={0} | all-to-all | bytes 131072 | tf_op jit(solution)/shard_map/all_to_all | solution.py:400
  26.1 0.0 copy-done
  26.1 0.2 image_sticks.1
  26.3 1.6 %collective-permute-start = (bf16[288,128]{1,0:T(8,128)(2,1)S(1)}, bf16[288,128]{1,0:T(8,128)(2,1)S(1)}, u32[]{:S(2)}, u32[]{:S(2)}) collective-permute-start(bf16[288,128]{1,0:T(8,128)(2,1)S(1)} %get-tuple-element.27), channel_id=1, source_target_pairs={{0,1},{1,0},{2,3},{3,2},{4,5},{5,4},{6,7},{7,6},{8,9},{9,8},{10,11... | collective-permute-start | bytes 221192 | tf_op jit(solution)/shard_map/ppermute | solution.py:405
  27.8 1.5 %collective-permute-start.1 = (bf16[288,128]{1,0:T(8,128)(2,1)S(1)}, bf16[288,128]{1,0:T(8,128)(2,1)S(1)}, u32[]{:S(2)}, u32[]{:S(2)}) collective-permute-start(bf16[288,128]{1,0:T(8,128)(2,1)S(1)} %get-tuple-element.27), channel_id=1, source_target_pairs={{0,2},{1,3},{2,0},{3,1},{4,6},{5,7},{6,4},{7,5},{8,10},{9,11},{10,... | collective-permute-start | bytes 221192 | tf_op jit(solution)/shard_map/ppermute | solution.py:405
  29.4 0.5 %collective-permute-start.2 = (bf16[288,128]{1,0:T(8,128)(2,1)S(1)}, bf16[288,128]{1,0:T(8,128)(2,1)S(1)}, u32[]{:S(2)}, u32[]{:S(2)}) collective-permute-start(bf16[288,128]{1,0:T(8,128)(2,1)S(1)} %get-tuple-element.27), channel_id=1, source_target_pairs={{0,3},{1,2},{2,1},{3,0},{4,7},{5,6},{6,5},{7,4},{8,11},{9,10},{10,... | collective-permute-start | bytes 221192 | tf_op jit(solution)/shard_map/ppermute | solution.py:405
  29.8 1.7 %bring.1 = bf16[128,72,128]{2,1,0:T(8,128)(2,1)S(1)} custom-call(f32[2,128]{1,0:T(2,128)S(1)} %get-tuple-element.28.after_ref.sums_ref, bf16[128,72,128]{2,1,0:T(8,128)(2,1)} %bitcast.12), custom_call_target="tpu_custom_call" | custom-call | tf_op jit(solution)/shard_map/bring/pallas_call | solution.py:100
  31.5 0.0 collective-permute-done
  31.5 1.5 %collective-permute-done.1 = bf16[288,128]{1,0:T(8,128)(2,1)S(1)} collective-permute-done((bf16[288,128]{1,0:T(8,128)(2,1)S(1)}, bf16[288,128]{1,0:T(8,128)(2,1)S(1)}, u32[]{:S(2)}, u32[]{:S(2)}) %collective-permute-start.1) | collective-permute-done | bytes 73760 | tf_op jit(solution)/shard_map/ppermute | solution.py:405
  33.0 1.6 %collective-permute-done.2 = bf16[288,128]{1,0:T(8,128)(2,1)S(1)} collective-permute-done((bf16[288,128]{1,0:T(8,128)(2,1)S(1)}, bf16[288,128]{1,0:T(8,128)(2,1)S(1)}, u32[]{:S(2)}, u32[]{:S(2)}) %collective-permute-start.2) | collective-permute-done | bytes 73760 | tf_op jit(solution)/shard_map/ppermute | solution.py:405
  34.6 0.7 %fusion.2.product_ref = f32[16,128]{1,0:T(8,128)S(1)} fusion(bf16[128,72,128]{2,1,0:T(8,128)(2,1)S(1)} %bring.1, bf16[16,72,128]{2,1,0:T(8,128)(2,1)S(1)} %bitcast.13), kind=kOutput, calls=%fused_computation.2 | convolution fusion | flops 37748736 | bytes 2662400 | tf_op jit(solution)/shard_map/dot_general | solution.py:409
  35.4 8.7 %all_to_all.17.copies_ref = f32[8,24,128]{2,1,0:T(8,128)S(1)} all-to-all(f32[8,24,128]{2,1,0:T(8,128)S(1)} %share.1), channel_id=1, replica_groups=mesh['pw'=8,'band'=4] {'pw'}, dimensions={0} | all-to-all | bytes 196608 | tf_op jit(solution)/shard_map/all_to_all | solution.py:418
  44.1 0.9 %finish.1 = (f32[144,128]{1,0:T(8,128)}, f32[2,4,64]{2,1,0:T(4,128)}, f32[2,4,64]{2,1,0:T(4,128)}) custom-call(s32[1]{0:T(128)} %bitcast.6.band_ref, f32[8,24,128]{2,1,0:T(8,128)S(1)} %all_to_all.17.copies_ref, f32[144,128]{1,0:T(8,128)S(1)} %get-tuple-element.31.image_ref, f32[144,128]{1,0:T(8,128)S(1)} %get-tuple-element.25.vector_ref), custom_call_target="tpu_custom_call" | custom-call | tf_op jit(solution)/shard_map/finish/pallas_call | solution.py:377
  (2 shorter events, 0.0 us)
Async XLA Ops:
  0.6 25.5 %copy-start = (bf16[288,256]{1,0:T(8,128)(2,1)S(1)}, bf16[288,256]{1,0:T(8,128)(2,1)}, u32[]{:S(2)}) copy-start(bf16[288,256]{1,0:T(8,128)(2,1)} %constant.22.clone.table_ref) | copy-start | bytes 442372
  26.3 5.2 %collective-permute-start = (bf16[288,128]{1,0:T(8,128)(2,1)S(1)}, bf16[288,128]{1,0:T(8,128)(2,1)S(1)}, u32[]{:S(2)}, u32[]{:S(2)}) collective-permute-start(bf16[288,128]{1,0:T(8,128)(2,1)S(1)} %get-tuple-element.27), channel_id=1, source_target_pairs={{0,1},{1,0},{2,3},{3,2},{4,5},{5,4},{6,7},{7,6},{8,9},{9,8},{10,11... | collective-permute-start | bytes 221192 | tf_op jit(solution)/shard_map/ppermute | solution.py:405
  27.8 5.1 %collective-permute-start.1 = (bf16[288,128]{1,0:T(8,128)(2,1)S(1)}, bf16[288,128]{1,0:T(8,128)(2,1)S(1)}, u32[]{:S(2)}, u32[]{:S(2)}) collective-permute-start(bf16[288,128]{1,0:T(8,128)(2,1)S(1)} %get-tuple-element.27), channel_id=1, source_target_pairs={{0,2},{1,3},{2,0},{3,1},{4,6},{5,7},{6,4},{7,5},{8,10},{9,11},{10,... | collective-permute-start | bytes 221192 | tf_op jit(solution)/shard_map/ppermute | solution.py:405
  29.4 5.3 %collective-permute-start.2 = (bf16[288,128]{1,0:T(8,128)(2,1)S(1)}, bf16[288,128]{1,0:T(8,128)(2,1)S(1)}, u32[]{:S(2)}, u32[]{:S(2)}) collective-permute-start(bf16[288,128]{1,0:T(8,128)(2,1)S(1)} %get-tuple-element.27), channel_id=1, source_target_pairs={{0,3},{1,2},{2,1},{3,0},{4,7},{5,6},{6,5},{7,4},{8,11},{9,10},{10,... | collective-permute-start | bytes 221192 | tf_op jit(solution)/shard_map/ppermute | solution.py:405

commit v5 on v3

--- a/solution.py
+++ b/solution.py
@@ -30,13 +30,13 @@
 
 
 def split(table, count):
-    pieces = []
+    pot_copy = []
     rest = np.asarray(table, np.float64)
     for _ in range(count):
         piece = rest.astype(jnp.bfloat16)
-        pieces.append(piece)
+        pot_copy.append(piece)
         rest = rest - piece.astype(np.float64)
-    return pieces
+    return pot_copy
 
 
 class Sizes:
@@ -72,7 +72,7 @@
     table = phases(z_freq, z_index, -1, sizes.grid) * real / float(sizes.grid**3)
     table = table.reshape(2 * sizes.depth, 2, sizes.groups, sizes.rows)
     table = table.transpose(0, 2, 1, 3).reshape(2 * sizes.depth, -1)
-    return np.concatenate(split(table, 3), 0)
+    return np.concatenate(split(table, 2), 0)
 
 
 def plane_tables(sizes):
@@ -197,24 +197,26 @@
     half = high_count * rows
 
     psi_bytes, other_bytes = (sum(array.nbytes for array in arrays) for arrays in ((psi_res,), (received, received, near)))
-    bring = psi_bytes + other_bytes < 3200000
+    fits = psi_bytes + other_bytes < 3200000
 
     def kernel(in_ref, yb_ref, *refs):
         *distant, out_ref = refs[:5]
         scratch = refs[5:]
-        if bring:
+        if fits:
             *distant, psi_far = refs[:5]
             out_ref, psi_ref, *scratch = refs[5:]
-        *near_refs, left_ref, hot_ref, a_ref, b_ref, sems = scratch
+            psi_copy = pltpu.make_async_copy(psi_far, psi_ref, scratch[-1].at[4])
+        *near_refs, left_ref, hot_ref, a_ref, b_ref, field_ref, sems = scratch
         xb_ref, pot_ref, xf_ref, yf_ref = near_refs
-        copies = [
-            pltpu.make_async_copy(source, target, sems.at[index])
-            for index, (source, target) in enumerate(zip(distant, near_refs, strict=True))
+        tables = [
+            pltpu.make_async_copy(distant[index], near_refs[index], sems.at[slot])
+            for slot, index in enumerate((0, 2, 3))
         ]
-        if bring:
-            copies.append(pltpu.make_async_copy(psi_far, psi_ref, sems.at[4]))
-        for copy in copies:
+        pot_copy = pltpu.make_async_copy(distant[1], pot_ref, sems.at[3])
+        for copy in (tables[0], pot_copy, *tables[1:]):
             copy.start()
+        if fits:
+            psi_copy.start()
 
         def relative(row):
             position = jnp.concatenate([in_ref[g, 2 * rows : 2 * rows + 16, :].astype(f32)[row : row + 1] for g in range(groups)], 0)
@@ -250,18 +252,20 @@
         for part in range(2):
             a_ref[part] = lines[:, part * grid : (part + 1) * grid]
 
-        def to_field(first):
+        tables[0].wait()
+        for first in range(0, rows, 2):
             high, low = [], []
             for plane in (first, first + 1):
                 lines = jnp.concatenate([a_ref[part, pl.ds(plane, box, stride=rows), :] for part in range(2)], 0)
                 high.append(lines.astype(bf16))
                 low.append((lines - high[-1].astype(f32)).astype(bf16))
             high, low = jnp.concatenate(high, 1), jnp.concatenate(low, 1)
-            field = jnp.dot(xb_ref[...], jnp.concatenate([high, high, low], 0), preferred_element_type=f32)
+            field_ref[first // 2] = jnp.dot(xb_ref[...], jnp.concatenate([high, high, low], 0), preferred_element_type=f32)
+        for copy in (pot_copy, tables[1], tables[2]):
+            copy.wait()
+        for first in range(0, rows, 2):
             weight = jnp.concatenate([pot_ref[first], pot_ref[first + 1]], 1)
-            return (field * jnp.concatenate([weight, weight], 0)).astype(bf16)
-
-        def from_field(first, field):
+            field = (field_ref[first // 2] * jnp.concatenate([weight, weight], 0)).astype(bf16)
             back = jnp.dot(xf_ref[...], field, preferred_element_type=f32)
             back = back[: 2 * box] + back[2 * box :]
             for index in range(2):
@@ -270,15 +274,6 @@
                         part * box : (part + 1) * box, index * grid : (index + 1) * grid
                     ]
 
-        for copy in copies[:3]:
-            copy.wait()
-        fields = [to_field(0)]
-        for first in range(0, rows, 2):
-            if first + 2 < rows:
-                fields.append(to_field(first + 2))
-            from_field(first, fields[first // 2])
-
-        copies[3].wait()
         lines = jnp.concatenate([b_ref[0], b_ref[1]], 1).astype(bf16)
         boxed = jnp.dot(lines, yf_ref[...], preferred_element_type=f32)
         boxed = boxed[:, : 2 * line] + boxed[:, 2 * line :]
@@ -304,10 +299,10 @@
                         piece = found[start : start + rows, (g - first) * local : (g - first + 1) * local]
                         total = total + jnp.where(highs[g] == float(high), piece, 0.0)
                     out_ref[g, part * rows : (part + 1) * rows, :] = total.astype(bf16)
-        for copy in copies[4:]:
-            copy.wait()
-
-    extra = (psi_res,) if bring else ()
+        if fits:
+            psi_copy.wait()
+
+    extra = (psi_res,) if fits else ()
     picked, *brought = call_on_chip(
         kernel,
         "apply_planes",
@@ -320,10 +315,11 @@
             pltpu.VMEM((columns, sticks), bf16),
             pltpu.VMEM((2, box * rows, grid), f32),
             pltpu.VMEM((2, box * rows, grid), f32),
+            pltpu.VMEM((rows // 2, 2 * grid, 2 * grid), f32),
             pltpu.SemaphoreType.DMA((5,)),
         ),
     )
-    return picked, brought[0] if bring else psi_res
+    return picked, brought[0] if fits else psi_res
 
 
 def image_sticks(sizes, columns, vector, positions):
@@ -332,7 +328,7 @@
 
     def kernel(table_ref, columns_ref, vector_ref, position_ref, image_ref, rounded_ref, sums_ref):
         product = jnp.dot(table_ref[...], columns_ref[...], preferred_element_type=f32)
-        applied = product[:height] + (product[height : 2 * height] + product[2 * height :])
+        applied = product[:height] + product[height:]
         vector = vector_ref[...]
         x_freq = signed_freq(position_ref[...] // grid, grid)
         y_freq = signed_freq(position_ref[...] % grid, grid)
@@ -370,17 +366,17 @@
 def finish(copies, image, vector, band, band_total, res_count):
     count = copies.shape[0]
     width = 2 * res_count
-    table = np.zeros((width, width), np.float32)
-    lane = np.arange(width)
-    table[lane, lane % 2 * res_count + lane // 2] = 1.0
-
-    def kernel(band_ref, table_ref, copies_ref, image_ref, vector_ref, residual_ref, ham_ref, inter_ref, total_ref):
+
+    def kernel(band_ref, copies_ref, image_ref, vector_ref, residual_ref, ham_ref, inter_ref, total_ref):
         total = copies_ref[0]
         for index in range(1, count):
             total = total + copies_ref[index]
         tail = jnp.sum(total[4 * band_total : 4 * band_total + 2], axis=1, keepdims=True)
         residual_ref[...] = image_ref[...] - (tail[0:1] / tail[1:2]) * vector_ref[...]
-        total_ref[...] = jnp.dot(total[: 4 * band_total], table_ref[...], precision=highest, preferred_element_type=f32)
+        source = lax.broadcasted_iota(jnp.int32, (width, width), 0)
+        target = lax.broadcasted_iota(jnp.int32, (width, width), 1)
+        table = jnp.where(target == source % 2 * res_count + source // 2, 1.0, 0.0)
+        total_ref[...] = jnp.dot(total[: 4 * band_total], table, precision=highest, preferred_element_type=f32)
         for column in range(band_total):
             source = column ^ band_ref[0]
             for index, out_ref in enumerate((inter_ref, ham_ref)):
@@ -390,12 +386,12 @@
                 out_ref[1, column : column + 1, :] = imag[:, :res_count] - real[:, res_count:]
 
     spec = pl.BlockSpec(memory_space=pltpu.VMEM)
-    operands = (jnp.asarray(table), copies, image, vector)
+    operands = (copies, image, vector)
     projection = jax.ShapeDtypeStruct((2, band_total, res_count), f32)
     return pl.pallas_call(
         kernel,
         out_shape=(jax.ShapeDtypeStruct(image.shape, f32), projection, projection),
-        in_specs=[pl.BlockSpec(memory_space=pltpu.SMEM)] + [spec] * 4,
+        in_specs=[pl.BlockSpec(memory_space=pltpu.SMEM)] + [spec] * 3,
         out_specs=(spec,) * 3,
         scratch_shapes=[pltpu.VMEM((4 * band_total, width), f32)],
         name="finish",

time: 45.1 us -> 44.1 us (0.978)
  Pallas kernels: 6.4 us -> 5.65 us
    pallas_call x4, Pallas kernels: 5.55 us -> 4.79 us  [call_on_chip(): pl.pallas_call(kernel, out_shape=tuple((pltpu.VMEM(shape, dtype) for shap...]
where the time goes in v5:
time: 44.1 us; the launch traced here: 43.9 us
  blocking collectives  29.5 us (67%)
  Pallas kernels  5.65 us (13%)
  waiting for transfers between devices  3.82 us (9%)
  starting transfers between devices  3.55 us (8%)
  matrix products  0.7 us (2%)
  between operations  0.67 us (2%)
    all_to_all x1, blocking collectives, shards(): lax.all_to_all(moving, 'pw', split_axis=0, concat_axis=0, tiled=True)  12.5 us
    all_to_all x1, blocking collectives, shards(): lax.all_to_all(copies, 'pw', split_axis=0, concat_axis=0, tiled=True)  8.7 us
    all_to_all x1, blocking collectives, shards(): lax.all_to_all(picked, 'pw', split_axis=0, concat_axis=0, tiled=True)  8.3 us
    pallas_call x4, Pallas kernels, call_on_chip(): pl.pallas_call(kernel, out_shape=tuple((pltpu.VMEM(shape, dtype) for shap...  4.79 us
    ppermute x3, waiting for transfers between devices, shards(): lax.ppermute(rounded, 'band', [(i, i ^ step) for i in range(band_total)])  3.82 us
    ppermute x3, starting transfers between devices, shards(): lax.ppermute(rounded, 'band', [(i, i ^ step) for i in range(band_total)])  3.55 us
  transfers between devices with their start and end apart: 3, of which 3 were waited for; matrix products, arithmetic and copies ran while one was open for 0% of the time, Pallas kernels for 0%

profile of v5, /device:TPU:0, one launch (start us, length us, event | category | flops | bytes accessed | tf_op | source)
XLA Modules:
  0.0 43.9 jit_solution(17283311285592531026)
XLA Ops:
  0.6 0.0 copy-start
  0.6 1.3 %spread_sticks.1 = (bf16[8,48,128]{2,1,0:T(8,128)(2,1)S(1)}, f32[144,128]{1,0:T(8,128)S(1)}, s32[1,128]{1,0:T(1,128)S(1)}, bf16[256,256]{1,0:T(8,128)(2,1)S(1)}) custom-call(f32[144,128]{1,0:T(8,128)} %bitcast.14, bf16[256,432]{1,0:T(8,128)(2,1)} %constant.21.clone.refs_1_, s32[1,128]{1,0:T(1,128)} %bitcast.15, bf16[256,256]{1,0:T(8,128)(2,1)} %constant.8.clone.refs_3_), custom_call_target="tpu_custom_call" | custom-call | tf_op jit(solution)/shard_map/spread_sticks/pallas_call | solution.py:100
  1.9 12.5 %all_to_all.15.in_ref = bf16[8,48,128]{2,1,0:T(8,128)(2,1)S(1)} all-to-all(bf16[8,48,128]{2,1,0:T(8,128)(2,1)S(1)} %get-tuple-element.17), channel_id=1, replica_groups=mesh['pw'=8,'band'=4] {'pw'}, dimensions={0} | all-to-all | bytes 196608 | tf_op jit(solution)/shard_map/all_to_all | solution.py:413
  14.4 3.3 %apply_planes.1 = (bf16[8,32,128]{2,1,0:T(8,128)(2,1)S(1)}, bf16[128,72,128]{2,1,0:T(8,128)(2,1)S(1)}) custom-call(bf16[8,48,128]{2,1,0:T(8,128)(2,1)S(1)} %all_to_all.15.in_ref, bf16[256,256]{1,0:T(8,128)(2,1)S(1)} %get-tuple-element.18.yb_ref, bf16[256,240]{1,0:T(8,128)(2,1)} %constant.18.clone.refs_0_, f32[16,128,128]{2,1,0:T(8,128)} %refs_1_.2, ...), custom_call_target="tpu_custom_call" | custom-call | tf_op jit(solution)/shard_map/apply_planes/pallas_call | solution.py:100
  17.7 8.3 %all_to_all.16 = bf16[8,32,128]{2,1,0:T(8,128)(2,1)S(1)} all-to-all(bf16[8,32,128]{2,1,0:T(8,128)(2,1)S(1)} %get-tuple-element.19), channel_id=1, replica_groups=mesh['pw'=8,'band'=4] {'pw'}, dimensions={0} | all-to-all | bytes 131072 | tf_op jit(solution)/shard_map/all_to_all | solution.py:415
  26.0 0.0 copy-done
  26.0 0.2 image_sticks.1
  26.2 2.5 %collective-permute-start.2 = (bf16[288,128]{1,0:T(8,128)(2,1)S(1)}, bf16[288,128]{1,0:T(8,128)(2,1)S(1)}, u32[]{:S(2)}, u32[]{:S(2)}) collective-permute-start(bf16[288,128]{1,0:T(8,128)(2,1)S(1)} %get-tuple-element.22), channel_id=1, source_target_pairs={{0,3},{1,2},{2,1},{3,0},{4,7},{5,6},{6,5},{7,4},{8,11},{9,10},{10,... | collective-permute-start | bytes 221192 | tf_op jit(solution)/shard_map/ppermute | solution.py:420
  28.7 0.5 %collective-permute-start.1 = (bf16[288,128]{1,0:T(8,128)(2,1)S(1)}, bf16[288,128]{1,0:T(8,128)(2,1)S(1)}, u32[]{:S(2)}, u32[]{:S(2)}) collective-permute-start(bf16[288,128]{1,0:T(8,128)(2,1)S(1)} %get-tuple-element.22), channel_id=1, source_target_pairs={{0,2},{1,3},{2,0},{3,1},{4,6},{5,7},{6,4},{7,5},{8,10},{9,11},{10,... | collective-permute-start | bytes 221192 | tf_op jit(solution)/shard_map/ppermute | solution.py:420
  29.2 0.5 %collective-permute-start = (bf16[288,128]{1,0:T(8,128)(2,1)S(1)}, bf16[288,128]{1,0:T(8,128)(2,1)S(1)}, u32[]{:S(2)}, u32[]{:S(2)}) collective-permute-start(bf16[288,128]{1,0:T(8,128)(2,1)S(1)} %get-tuple-element.22), channel_id=1, source_target_pairs={{0,1},{1,0},{2,3},{3,2},{4,5},{5,4},{6,7},{7,6},{8,9},{9,8},{10,11... | collective-permute-start | bytes 221192 | tf_op jit(solution)/shard_map/ppermute | solution.py:420
  29.7 1.9 %collective-permute-done.2 = bf16[288,128]{1,0:T(8,128)(2,1)S(1)} collective-permute-done((bf16[288,128]{1,0:T(8,128)(2,1)S(1)}, bf16[288,128]{1,0:T(8,128)(2,1)S(1)}, u32[]{:S(2)}, u32[]{:S(2)}) %collective-permute-start.2) | collective-permute-done | bytes 73760 | tf_op jit(solution)/shard_map/ppermute | solution.py:420
  31.6 1.4 %collective-permute-done.1 = bf16[288,128]{1,0:T(8,128)(2,1)S(1)} collective-permute-done((bf16[288,128]{1,0:T(8,128)(2,1)S(1)}, bf16[288,128]{1,0:T(8,128)(2,1)S(1)}, u32[]{:S(2)}, u32[]{:S(2)}) %collective-permute-start.1) | collective-permute-done | bytes 73760 | tf_op jit(solution)/shard_map/ppermute | solution.py:420
  33.0 0.5 %collective-permute-done = bf16[288,128]{1,0:T(8,128)(2,1)S(1)} collective-permute-done((bf16[288,128]{1,0:T(8,128)(2,1)S(1)}, bf16[288,128]{1,0:T(8,128)(2,1)S(1)}, u32[]{:S(2)}, u32[]{:S(2)}) %collective-permute-start) | collective-permute-done | bytes 73760 | tf_op jit(solution)/shard_map/ppermute | solution.py:420
  33.6 0.7 %fusion.2.product_ref = f32[16,128]{1,0:T(8,128)S(1)} fusion(bf16[128,72,128]{2,1,0:T(8,128)(2,1)S(1)} %get-tuple-element.23, bf16[16,72,128]{2,1,0:T(8,128)(2,1)S(1)} %bitcast.13), kind=kOutput, calls=%fused_computation.2 | convolution fusion | flops 37748736 | bytes 2662400 | tf_op jit(solution)/shard_map/dot_general | solution.py:423
  34.3 8.7 %all_to_all.17.copies_ref = f32[8,24,128]{2,1,0:T(8,128)S(1)} all-to-all(f32[8,24,128]{2,1,0:T(8,128)S(1)} %share.1), channel_id=1, replica_groups=mesh['pw'=8,'band'=4] {'pw'}, dimensions={0} | all-to-all | bytes 196608 | tf_op jit(solution)/shard_map/all_to_all | solution.py:432
  43.0 0.9 %finish.1 = (f32[144,128]{1,0:T(8,128)}, f32[2,4,64]{2,1,0:T(4,128)}, f32[2,4,64]{2,1,0:T(4,128)}) custom-call(s32[1]{0:T(128)} %bitcast.6.band_ref, f32[8,24,128]{2,1,0:T(8,128)S(1)} %all_to_all.17.copies_ref, f32[144,128]{1,0:T(8,128)S(1)} %get-tuple-element.27.image_ref, f32[144,128]{1,0:T(8,128)S(1)} %get-tuple-element.20.vector_ref), custom_call_target="tpu_custom_call" | custom-call | tf_op jit(solution)/shard_map/finish/pallas_call | solution.py:391
  (2 shorter events, 0.0 us)
Async XLA Ops:
  0.6 25.4 %copy-start = (bf16[288,256]{1,0:T(8,128)(2,1)S(1)}, bf16[288,256]{1,0:T(8,128)(2,1)}, u32[]{:S(2)}) copy-start(bf16[288,256]{1,0:T(8,128)(2,1)} %constant.22.clone.table_ref) | copy-start | bytes 442372
  26.2 5.4 %collective-permute-start.2 = (bf16[288,128]{1,0:T(8,128)(2,1)S(1)}, bf16[288,128]{1,0:T(8,128)(2,1)S(1)}, u32[]{:S(2)}, u32[]{:S(2)}) collective-permute-start(bf16[288,128]{1,0:T(8,128)(2,1)S(1)} %get-tuple-element.22), channel_id=1, source_target_pairs={{0,3},{1,2},{2,1},{3,0},{4,7},{5,6},{6,5},{7,4},{8,11},{9,10},{10,... | collective-permute-start | bytes 221192 | tf_op jit(solution)/shard_map/ppermute | solution.py:420
  28.7 4.4 %collective-permute-start.1 = (bf16[288,128]{1,0:T(8,128)(2,1)S(1)}, bf16[288,128]{1,0:T(8,128)(2,1)S(1)}, u32[]{:S(2)}, u32[]{:S(2)}) collective-permute-start(bf16[288,128]{1,0:T(8,128)(2,1)S(1)} %get-tuple-element.22), channel_id=1, source_target_pairs={{0,2},{1,3},{2,0},{3,1},{4,6},{5,7},{6,4},{7,5},{8,10},{9,11},{10,... | collective-permute-start | bytes 221192 | tf_op jit(solution)/shard_map/ppermute | solution.py:420
  29.2 4.4 %collective-permute-start = (bf16[288,128]{1,0:T(8,128)(2,1)S(1)}, bf16[288,128]{1,0:T(8,128)(2,1)S(1)}, u32[]{:S(2)}, u32[]{:S(2)}) collective-permute-start(bf16[288,128]{1,0:T(8,128)(2,1)S(1)} %get-tuple-element.22), channel_id=1, source_target_pairs={{0,1},{1,0},{2,3},{3,2},{4,5},{5,4},{6,7},{7,6},{8,9},{9,8},{10,11... | collective-permute-start | bytes 221192 | tf_op jit(solution)/shard_map/ppermute | solution.py:420

commit v6 on v5

--- a/solution.py
+++ b/solution.py
@@ -131,7 +131,7 @@
         columns = jnp.dot(table_ref[...], stacked, preferred_element_type=f32)
         x_pos = (position_ref[...] // sizes.grid).astype(f32)
         y_pos = (position_ref[...] % sizes.grid).astype(f32)
-        row = lax.broadcasted_iota(jnp.int32, (16, sizes.sticks_local), 0)
+        row = lax.broadcasted_iota(jnp.int32, (8, sizes.sticks_local), 0)
         tail = jnp.where(row == 0, x_pos, jnp.where(row == 1, y_pos, 0.0)).astype(bf16)
         for group in range(sizes.groups):
             out_ref[group, 0:block, :] = columns[group * block : (group + 1) * block].astype(bf16)
@@ -143,7 +143,7 @@
         kernel,
         "spread_sticks",
         (),
-        (((sizes.groups, block + 16, sizes.sticks_local), bf16), *[(array.shape, array.dtype) for array in kept]),
+        (((sizes.groups, block + 8, sizes.sticks_local), bf16), *[(array.shape, array.dtype) for array in kept]),
         far,
         [pltpu.VMEM(z_table.shape, z_table.dtype), pltpu.SemaphoreType.DMA((len(far),))],
     )
@@ -219,7 +219,7 @@
             psi_copy.start()
 
         def relative(row):
-            position = jnp.concatenate([in_ref[g, 2 * rows : 2 * rows + 16, :].astype(f32)[row : row + 1] for g in range(groups)], 0)
+            position = jnp.concatenate([in_ref[g, 2 * rows : 2 * rows + 8, :].astype(f32)[row : row + 1] for g in range(groups)], 0)
             moved = position - anchor_of(position, grid) + float(box // 2)
             moved = jnp.where(moved < 0, moved + float(grid), moved)
             return jnp.where(moved >= float(grid), moved - float(grid), moved)
@@ -352,38 +352,44 @@
 
 def share(product, sums, groups):
     count, width = product.shape
-    height = round_up(count + 2, 8)
-
-    def kernel(product_ref, sums_ref, out_ref):
-        fill = jnp.zeros((height - count - 2, width), f32)
-        partial = jnp.concatenate([product_ref[...], sums_ref[...], fill], 0)
+    half = width // 2
+    height = round_up(count // 2 + 2, 8)
+
+    def kernel(product_ref, sums_ref, out_ref, sorted_ref):
+        source = lax.broadcasted_iota(jnp.int32, (width, width), 0)
+        target = lax.broadcasted_iota(jnp.int32, (width, width), 1)
+        table = jnp.where(target == source % 2 * half + source // 2, 1.0, 0.0)
+        sorted_ref[...] = jnp.dot(product_ref[...], table, precision=highest, preferred_element_type=f32)
+        real = sorted_ref[pl.ds(0, count // 2, stride=2), :]
+        imag = sorted_ref[pl.ds(1, count // 2, stride=2), :]
+        low = lax.broadcasted_iota(jnp.int32, real.shape, 1) < half
+        joined = jnp.where(low, real, -real) + pltpu.roll(imag, half, 1)
+        fill = jnp.zeros((height - count // 2 - 2, width), f32)
+        partial = jnp.concatenate([joined, sums_ref[...], fill], 0)
         for group in range(groups):
             out_ref[group] = partial
 
-    return call_on_chip(kernel, "share", (product, sums), (((groups, height, width), f32),))[0]
+    return call_on_chip(
+        kernel, "share", (product, sums), (((groups, height, width), f32),), scratch=(pltpu.VMEM((count, width), f32),)
+    )[0]
 
 
 def finish(copies, image, vector, band, band_total, res_count):
-    count = copies.shape[0]
-    width = 2 * res_count
+    count, height, width = copies.shape
 
     def kernel(band_ref, copies_ref, image_ref, vector_ref, residual_ref, ham_ref, inter_ref, total_ref):
         total = copies_ref[0]
         for index in range(1, count):
             total = total + copies_ref[index]
-        tail = jnp.sum(total[4 * band_total : 4 * band_total + 2], axis=1, keepdims=True)
+        tail = jnp.sum(total[2 * band_total : 2 * band_total + 2], axis=1, keepdims=True)
         residual_ref[...] = image_ref[...] - (tail[0:1] / tail[1:2]) * vector_ref[...]
-        source = lax.broadcasted_iota(jnp.int32, (width, width), 0)
-        target = lax.broadcasted_iota(jnp.int32, (width, width), 1)
-        table = jnp.where(target == source % 2 * res_count + source // 2, 1.0, 0.0)
-        total_ref[...] = jnp.dot(total[: 4 * band_total], table, precision=highest, preferred_element_type=f32)
+        total_ref[...] = total
         for column in range(band_total):
             source = column ^ band_ref[0]
             for index, out_ref in enumerate((inter_ref, ham_ref)):
-                real = total_ref[pl.ds(source * 4 + index * 2, 1), :]
-                imag = total_ref[pl.ds(source * 4 + index * 2 + 1, 1), :]
-                out_ref[0, column : column + 1, :] = real[:, :res_count] + imag[:, res_count:]
-                out_ref[1, column : column + 1, :] = imag[:, :res_count] - real[:, res_count:]
+                row = total_ref[pl.ds(source * 2 + index, 1), :]
+                for part in range(2):
+                    out_ref[part, column : column + 1, :] = row[:, part * res_count : (part + 1) * res_count]
 
     spec = pl.BlockSpec(memory_space=pltpu.VMEM)
     operands = (copies, image, vector)
@@ -393,7 +399,7 @@
         out_shape=(jax.ShapeDtypeStruct(image.shape, f32), projection, projection),
         in_specs=[pl.BlockSpec(memory_space=pltpu.SMEM)] + [spec] * 3,
         out_specs=(spec,) * 3,
-        scratch_shapes=[pltpu.VMEM((4 * band_total, width), f32)],
+        scratch_shapes=[pltpu.VMEM((height, width), f32)],
         name="finish",
     )(band, *[pltpu.with_memory_space_constraint(operand, pltpu.VMEM) for operand in operands])
 

time: 44.1 us -> 43.6 us (0.989)
  blocking collectives: 29.5 us -> 28.8 us
where the time goes in v6:
time: 43.6 us; the launch traced here: 43.4 us
  blocking collectives  28.8 us (66%)
  Pallas kernels  5.8 us (13%)
  waiting for transfers between devices  3.81 us (9%)
  starting transfers between devices  3.55 us (8%)
  matrix products  0.7 us (2%)
  between operations  0.67 us (2%)
    all_to_all x1, blocking collectives, shards(): lax.all_to_all(moving, 'pw', split_axis=0, concat_axis=0, tiled=True)  12.2 us
    all_to_all x1, blocking collectives, shards(): lax.all_to_all(picked, 'pw', split_axis=0, concat_axis=0, tiled=True)  8.3 us
    all_to_all x1, blocking collectives, shards(): lax.all_to_all(copies, 'pw', split_axis=0, concat_axis=0, tiled=True)  8.3 us
    pallas_call x4, Pallas kernels, call_on_chip(): pl.pallas_call(kernel, out_shape=tuple((pltpu.VMEM(shape, dtype) for shap...  5.03 us
    ppermute x3, waiting for transfers between devices, shards(): lax.ppermute(rounded, 'band', [(i, i ^ step) for i in range(band_total)])  3.81 us
    ppermute x3, starting transfers between devices, shards(): lax.ppermute(rounded, 'band', [(i, i ^ step) for i in range(band_total)])  3.55 us
  transfers between devices with their start and end apart: 3, of which 3 were waited for; matrix products, arithmetic and copies ran while one was open for 0% of the time, Pallas kernels for 0%

profile of v6, /device:TPU:0, one launch (start us, length us, event | category | flops | bytes accessed | tf_op | source)
XLA Modules:
  0.0 43.4 jit_solution(6012419179940352487)
XLA Ops:
  0.6 0.0 copy-start
  0.6 1.3 %spread_sticks.1 = (bf16[8,40,128]{2,1,0:T(8,128)(2,1)S(1)}, f32[144,128]{1,0:T(8,128)S(1)}, s32[1,128]{1,0:T(1,128)S(1)}, bf16[256,256]{1,0:T(8,128)(2,1)S(1)}) custom-call(f32[144,128]{1,0:T(8,128)} %bitcast.14, bf16[256,432]{1,0:T(8,128)(2,1)} %constant.21.clone.refs_1_, s32[1,128]{1,0:T(1,128)} %bitcast.15, bf16[256,256]{1,0:T(8,128)(2,1)} %constant.8.clone.refs_3_), custom_call_target="tpu_custom_call" | custom-call | tf_op jit(solution)/shard_map/spread_sticks/pallas_call | solution.py:100
  1.9 12.2 %all_to_all.15.in_ref = bf16[8,40,128]{2,1,0:T(8,128)(2,1)S(1)} all-to-all(bf16[8,40,128]{2,1,0:T(8,128)(2,1)S(1)} %get-tuple-element.17), channel_id=1, replica_groups=mesh['pw'=8,'band'=4] {'pw'}, dimensions={0} | all-to-all | bytes 163840 | tf_op jit(solution)/shard_map/all_to_all | solution.py:419
  14.2 3.3 %apply_planes.1 = (bf16[8,32,128]{2,1,0:T(8,128)(2,1)S(1)}, bf16[128,72,128]{2,1,0:T(8,128)(2,1)S(1)}) custom-call(bf16[8,40,128]{2,1,0:T(8,128)(2,1)S(1)} %all_to_all.15.in_ref, bf16[256,256]{1,0:T(8,128)(2,1)S(1)} %get-tuple-element.18.yb_ref, bf16[256,240]{1,0:T(8,128)(2,1)} %constant.18.clone.refs_0_, f32[16,128,128]{2,1,0:T(8,128)} %refs_1_.2, ...), custom_call_target="tpu_custom_call" | custom-call | tf_op jit(solution)/shard_map/apply_planes/pallas_call | solution.py:100
  17.5 8.3 %all_to_all.16 = bf16[8,32,128]{2,1,0:T(8,128)(2,1)S(1)} all-to-all(bf16[8,32,128]{2,1,0:T(8,128)(2,1)S(1)} %get-tuple-element.19), channel_id=1, replica_groups=mesh['pw'=8,'band'=4] {'pw'}, dimensions={0} | all-to-all | bytes 131072 | tf_op jit(solution)/shard_map/all_to_all | solution.py:421
  25.8 0.0 copy-done
  25.8 0.2 image_sticks.1
  26.0 2.5 %collective-permute-start.2 = (bf16[288,128]{1,0:T(8,128)(2,1)S(1)}, bf16[288,128]{1,0:T(8,128)(2,1)S(1)}, u32[]{:S(2)}, u32[]{:S(2)}) collective-permute-start(bf16[288,128]{1,0:T(8,128)(2,1)S(1)} %get-tuple-element.22), channel_id=1, source_target_pairs={{0,3},{1,2},{2,1},{3,0},{4,7},{5,6},{6,5},{7,4},{8,11},{9,10},{10,... | collective-permute-start | bytes 221192 | tf_op jit(solution)/shard_map/ppermute | solution.py:426
  28.5 0.5 %collective-permute-start.1 = (bf16[288,128]{1,0:T(8,128)(2,1)S(1)}, bf16[288,128]{1,0:T(8,128)(2,1)S(1)}, u32[]{:S(2)}, u32[]{:S(2)}) collective-permute-start(bf16[288,128]{1,0:T(8,128)(2,1)S(1)} %get-tuple-element.22), channel_id=1, source_target_pairs={{0,2},{1,3},{2,0},{3,1},{4,6},{5,7},{6,4},{7,5},{8,10},{9,11},{10,... | collective-permute-start | bytes 221192 | tf_op jit(solution)/shard_map/ppermute | solution.py:426
  29.0 0.5 %collective-permute-start = (bf16[288,128]{1,0:T(8,128)(2,1)S(1)}, bf16[288,128]{1,0:T(8,128)(2,1)S(1)}, u32[]{:S(2)}, u32[]{:S(2)}) collective-permute-start(bf16[288,128]{1,0:T(8,128)(2,1)S(1)} %get-tuple-element.22), channel_id=1, source_target_pairs={{0,1},{1,0},{2,3},{3,2},{4,5},{5,4},{6,7},{7,6},{8,9},{9,8},{10,11... | collective-permute-start | bytes 221192 | tf_op jit(solution)/shard_map/ppermute | solution.py:426
  29.5 1.9 %collective-permute-done.2 = bf16[288,128]{1,0:T(8,128)(2,1)S(1)} collective-permute-done((bf16[288,128]{1,0:T(8,128)(2,1)S(1)}, bf16[288,128]{1,0:T(8,128)(2,1)S(1)}, u32[]{:S(2)}, u32[]{:S(2)}) %collective-permute-start.2) | collective-permute-done | bytes 73760 | tf_op jit(solution)/shard_map/ppermute | solution.py:426
  31.4 1.4 %collective-permute-done.1 = bf16[288,128]{1,0:T(8,128)(2,1)S(1)} collective-permute-done((bf16[288,128]{1,0:T(8,128)(2,1)S(1)}, bf16[288,128]{1,0:T(8,128)(2,1)S(1)}, u32[]{:S(2)}, u32[]{:S(2)}) %collective-permute-start.1) | collective-permute-done | bytes 73760 | tf_op jit(solution)/shard_map/ppermute | solution.py:426
  32.8 0.5 %collective-permute-done = bf16[288,128]{1,0:T(8,128)(2,1)S(1)} collective-permute-done((bf16[288,128]{1,0:T(8,128)(2,1)S(1)}, bf16[288,128]{1,0:T(8,128)(2,1)S(1)}, u32[]{:S(2)}, u32[]{:S(2)}) %collective-permute-start) | collective-permute-done | bytes 73760 | tf_op jit(solution)/shard_map/ppermute | solution.py:426
  33.4 0.7 %fusion.2.product_ref = f32[16,128]{1,0:T(8,128)S(1)} fusion(bf16[128,72,128]{2,1,0:T(8,128)(2,1)S(1)} %get-tuple-element.23, bf16[16,72,128]{2,1,0:T(8,128)(2,1)S(1)} %bitcast.13), kind=kOutput, calls=%fused_computation.2 | convolution fusion | flops 37748736 | bytes 2662400 | tf_op jit(solution)/shard_map/dot_general | solution.py:429
  34.1 0.3 share.1
  34.3 8.3 %all_to_all.17.copies_ref = f32[8,16,128]{2,1,0:T(8,128)S(1)} all-to-all(f32[8,16,128]{2,1,0:T(8,128)S(1)} %share.1), channel_id=1, replica_groups=mesh['pw'=8,'band'=4] {'pw'}, dimensions={0} | all-to-all | bytes 131072 | tf_op jit(solution)/shard_map/all_to_all | solution.py:438
  42.6 0.8 %finish.1 = (f32[144,128]{1,0:T(8,128)}, f32[2,4,64]{2,1,0:T(4,128)}, f32[2,4,64]{2,1,0:T(4,128)}) custom-call(s32[1]{0:T(128)} %bitcast.6.band_ref, f32[8,16,128]{2,1,0:T(8,128)S(1)} %all_to_all.17.copies_ref, f32[144,128]{1,0:T(8,128)S(1)} %get-tuple-element.27.image_ref, f32[144,128]{1,0:T(8,128)S(1)} %get-tuple-element.20.vector_ref), custom_call_target="tpu_custom_call" | custom-call | tf_op jit(solution)/shard_map/finish/pallas_call | solution.py:397
  (1 shorter events, 0.0 us)
Async XLA Ops:
  0.6 25.1 %copy-start = (bf16[288,256]{1,0:T(8,128)(2,1)S(1)}, bf16[288,256]{1,0:T(8,128)(2,1)}, u32[]{:S(2)}) copy-start(bf16[288,256]{1,0:T(8,128)(2,1)} %constant.22.clone.table_ref) | copy-start | bytes 442372
  26.0 5.4 %collective-permute-start.2 = (bf16[288,128]{1,0:T(8,128)(2,1)S(1)}, bf16[288,128]{1,0:T(8,128)(2,1)S(1)}, u32[]{:S(2)}, u32[]{:S(2)}) collective-permute-start(bf16[288,128]{1,0:T(8,128)(2,1)S(1)} %get-tuple-element.22), channel_id=1, source_target_pairs={{0,3},{1,2},{2,1},{3,0},{4,7},{5,6},{6,5},{7,4},{8,11},{9,10},{10,... | collective-permute-start | bytes 221192 | tf_op jit(solution)/shard_map/ppermute | solution.py:426
  28.5 4.4 %collective-permute-start.1 = (bf16[288,128]{1,0:T(8,128)(2,1)S(1)}, bf16[288,128]{1,0:T(8,128)(2,1)S(1)}, u32[]{:S(2)}, u32[]{:S(2)}) collective-permute-start(bf16[288,128]{1,0:T(8,128)(2,1)S(1)} %get-tuple-element.22), channel_id=1, source_target_pairs={{0,2},{1,3},{2,0},{3,1},{4,6},{5,7},{6,4},{7,5},{8,10},{9,11},{10,... | collective-permute-start | bytes 221192 | tf_op jit(solution)/shard_map/ppermute | solution.py:426
  29.0 4.4 %collective-permute-start = (bf16[288,128]{1,0:T(8,128)(2,1)S(1)}, bf16[288,128]{1,0:T(8,128)(2,1)S(1)}, u32[]{:S(2)}, u32[]{:S(2)}) collective-permute-start(bf16[288,128]{1,0:T(8,128)(2,1)S(1)} %get-tuple-element.22), channel_id=1, source_target_pairs={{0,1},{1,0},{2,3},{3,2},{4,5},{5,4},{6,7},{7,6},{8,9},{9,8},{10,11... | collective-permute-start | bytes 221192 | tf_op jit(solution)/shard_map/ppermute | solution.py:426

commit v7 on v6

--- a/solution.py
+++ b/solution.py
@@ -196,6 +196,7 @@
     columns = low_count * line
     half = high_count * rows
 
+    bands = psi_res.shape[0]
     psi_bytes, other_bytes = (sum(array.nbytes for array in arrays) for arrays in ((psi_res,), (received, received, near)))
     fits = psi_bytes + other_bytes < 3200000
 
@@ -205,7 +206,12 @@
         if fits:
             *distant, psi_far = refs[:5]
             out_ref, psi_ref, *scratch = refs[5:]
-            psi_copy = pltpu.make_async_copy(psi_far, psi_ref, scratch[-1].at[4])
+            psi_copies = [
+                pltpu.make_async_copy(
+                    psi_far.at[:, part], psi_ref.at[part * bands : (part + 1) * bands], scratch[-1].at[4 + part]
+                )
+                for part in range(2)
+            ]
         *near_refs, left_ref, hot_ref, a_ref, b_ref, field_ref, sems = scratch
         xb_ref, pot_ref, xf_ref, yf_ref = near_refs
         tables = [
@@ -216,7 +222,8 @@
         for copy in (tables[0], pot_copy, *tables[1:]):
             copy.start()
         if fits:
-            psi_copy.start()
+            for copy in psi_copies:
+                copy.start()
 
         def relative(row):
             position = jnp.concatenate([in_ref[g, 2 * rows : 2 * rows + 8, :].astype(f32)[row : row + 1] for g in range(groups)], 0)
@@ -300,14 +307,15 @@
                         total = total + jnp.where(highs[g] == float(high), piece, 0.0)
                     out_ref[g, part * rows : (part + 1) * rows, :] = total.astype(bf16)
         if fits:
-            psi_copy.wait()
+            for copy in psi_copies:
+                copy.wait()
 
     extra = (psi_res,) if fits else ()
     picked, *brought = call_on_chip(
         kernel,
         "apply_planes",
         (received, near),
-        (((groups, 2 * rows, local), bf16), *[(array.shape, array.dtype) for array in extra]),
+        (((groups, 2 * rows, local), bf16), *[((2 * bands, *array.shape[2:]), array.dtype) for array in extra]),
         (*later, *extra),
         (
             *[pltpu.VMEM(array.shape, array.dtype) for array in later],
@@ -316,10 +324,12 @@
             pltpu.VMEM((2, box * rows, grid), f32),
             pltpu.VMEM((2, box * rows, grid), f32),
             pltpu.VMEM((rows // 2, 2 * grid, 2 * grid), f32),
-            pltpu.SemaphoreType.DMA((5,)),
+            pltpu.SemaphoreType.DMA((6,)),
         ),
     )
-    return picked, brought[0] if fits else psi_res
+    if fits:
+        return picked, brought[0]
+    return picked, jnp.transpose(psi_res, (1, 0, 2, 3)).reshape(2 * bands, *psi_res.shape[2:])
 
 
 def image_sticks(sizes, columns, vector, positions):
@@ -355,13 +365,9 @@
     half = width // 2
     height = round_up(count // 2 + 2, 8)
 
-    def kernel(product_ref, sums_ref, out_ref, sorted_ref):
-        source = lax.broadcasted_iota(jnp.int32, (width, width), 0)
-        target = lax.broadcasted_iota(jnp.int32, (width, width), 1)
-        table = jnp.where(target == source % 2 * half + source // 2, 1.0, 0.0)
-        sorted_ref[...] = jnp.dot(product_ref[...], table, precision=highest, preferred_element_type=f32)
-        real = sorted_ref[pl.ds(0, count // 2, stride=2), :]
-        imag = sorted_ref[pl.ds(1, count // 2, stride=2), :]
+    def kernel(product_ref, sums_ref, out_ref):
+        real = product_ref[pl.ds(0, count // 2, stride=2), :]
+        imag = product_ref[pl.ds(1, count // 2, stride=2), :]
         low = lax.broadcasted_iota(jnp.int32, real.shape, 1) < half
         joined = jnp.where(low, real, -real) + pltpu.roll(imag, half, 1)
         fill = jnp.zeros((height - count // 2 - 2, width), f32)
@@ -369,9 +375,7 @@
         for group in range(groups):
             out_ref[group] = partial
 
-    return call_on_chip(
-        kernel, "share", (product, sums), (((groups, height, width), f32),), scratch=(pltpu.VMEM((count, width), f32),)
-    )[0]
+    return call_on_chip(kernel, "share", (product, sums), (((groups, height, width), f32),))[0]
 
 
 def finish(copies, image, vector, band, band_total, res_count):
@@ -417,7 +421,7 @@
     moving, vector, positions, y_back = spread_sticks(sizes, vector, stick_xy, y_back)
     later = (x_back, potential, x_forward, y_forward)
     moving = lax.all_to_all(moving, "pw", split_axis=0, concat_axis=0, tiled=True)
-    picked, psi_near = apply_planes(sizes, moving, y_back, later, psi_res.reshape(2 * res_count, stick_depth, sticks_local))
+    picked, psi_near = apply_planes(sizes, moving, y_back, later, psi_res)
     picked = lax.all_to_all(picked, "pw", split_axis=0, concat_axis=0, tiled=True)
     picked = picked.reshape(2 * sizes.rows * groups, sticks_local)
     image, rounded, sums = image_sticks(sizes, picked, vector, positions)

time: 43.6 us -> 43.5 us (level)
  no operation moved by 1% of the time
where the time goes in v7:
time: 43.5 us; the launch traced here: 43.2 us
  blocking collectives  28.8 us (66%)
  Pallas kernels  5.62 us (13%)
  waiting for transfers between devices  3.81 us (9%)
  starting transfers between devices  3.55 us (8%)
  matrix products  0.7 us (2%)
  between operations  0.67 us (2%)
    all_to_all x1, blocking collectives, shards(): lax.all_to_all(moving, 'pw', split_axis=0, concat_axis=0, tiled=True)  12.2 us
    all_to_all x1, blocking collectives, shards(): lax.all_to_all(copies, 'pw', split_axis=0, concat_axis=0, tiled=True)  8.31 us
    all_to_all x1, blocking collectives, shards(): lax.all_to_all(picked, 'pw', split_axis=0, concat_axis=0, tiled=True)  8.3 us
    pallas_call x4, Pallas kernels, call_on_chip(): pl.pallas_call(kernel, out_shape=tuple((pltpu.VMEM(shape, dtype) for shap...  4.85 us
    ppermute x3, waiting for transfers between devices, shards(): lax.ppermute(rounded, 'band', [(i, i ^ step) for i in range(band_total)])  3.81 us
    ppermute x3, starting transfers between devices, shards(): lax.ppermute(rounded, 'band', [(i, i ^ step) for i in range(band_total)])  3.55 us
  transfers between devices with their start and end apart: 3, of which 3 were waited for; matrix products, arithmetic and copies ran while one was open for 0% of the time, Pallas kernels for 0%

profile of v7, /device:TPU:0, one launch (start us, length us, event | category | flops | bytes accessed | tf_op | source)
XLA Modules:
  0.0 43.2 jit_solution(343443722319654703)
XLA Ops:
  0.6 0.0 copy-start
  0.6 1.3 %spread_sticks.1 = (bf16[8,40,128]{2,1,0:T(8,128)(2,1)S(1)}, f32[144,128]{1,0:T(8,128)S(1)}, s32[1,128]{1,0:T(1,128)S(1)}, bf16[256,256]{1,0:T(8,128)(2,1)S(1)}) custom-call(f32[144,128]{1,0:T(8,128)} %bitcast.12, bf16[256,432]{1,0:T(8,128)(2,1)} %constant.21.clone.refs_1_, s32[1,128]{1,0:T(1,128)} %bitcast.13, bf16[256,256]{1,0:T(8,128)(2,1)} %constant.8.clone.refs_3_), custom_call_target="tpu_custom_call" | custom-call | tf_op jit(solution)/shard_map/spread_sticks/pallas_call | solution.py:100
  1.9 12.2 %all_to_all.15.in_ref = bf16[8,40,128]{2,1,0:T(8,128)(2,1)S(1)} all-to-all(bf16[8,40,128]{2,1,0:T(8,128)(2,1)S(1)} %get-tuple-element.17), channel_id=1, replica_groups=mesh['pw'=8,'band'=4] {'pw'}, dimensions={0} | all-to-all | bytes 163840 | tf_op jit(solution)/shard_map/all_to_all | solution.py:423
  14.2 3.3 %apply_planes.1 = (bf16[8,32,128]{2,1,0:T(8,128)(2,1)S(1)}, bf16[128,72,128]{2,1,0:T(8,128)(2,1)S(1)}) custom-call(bf16[8,40,128]{2,1,0:T(8,128)(2,1)S(1)} %all_to_all.15.in_ref, bf16[256,256]{1,0:T(8,128)(2,1)S(1)} %get-tuple-element.18.yb_ref, bf16[256,240]{1,0:T(8,128)(2,1)} %constant.18.clone.refs_0_, f32[16,128,128]{2,1,0:T(8,128)} %refs_1_.2, ...), custom_call_target="tpu_custom_call" | custom-call | tf_op jit(solution)/shard_map/apply_planes/pallas_call | solution.py:100
  17.5 8.3 %all_to_all.16 = bf16[8,32,128]{2,1,0:T(8,128)(2,1)S(1)} all-to-all(bf16[8,32,128]{2,1,0:T(8,128)(2,1)S(1)} %get-tuple-element.19), channel_id=1, replica_groups=mesh['pw'=8,'band'=4] {'pw'}, dimensions={0} | all-to-all | bytes 131072 | tf_op jit(solution)/shard_map/all_to_all | solution.py:425
  25.8 0.0 copy-done
  25.8 0.2 image_sticks.1
  26.0 2.5 %collective-permute-start.2 = (bf16[288,128]{1,0:T(8,128)(2,1)S(1)}, bf16[288,128]{1,0:T(8,128)(2,1)S(1)}, u32[]{:S(2)}, u32[]{:S(2)}) collective-permute-start(bf16[288,128]{1,0:T(8,128)(2,1)S(1)} %get-tuple-element.22), channel_id=1, source_target_pairs={{0,3},{1,2},{2,1},{3,0},{4,7},{5,6},{6,5},{7,4},{8,11},{9,10},{10,... | collective-permute-start | bytes 221192 | tf_op jit(solution)/shard_map/ppermute | solution.py:430
  28.5 0.5 %collective-permute-start.1 = (bf16[288,128]{1,0:T(8,128)(2,1)S(1)}, bf16[288,128]{1,0:T(8,128)(2,1)S(1)}, u32[]{:S(2)}, u32[]{:S(2)}) collective-permute-start(bf16[288,128]{1,0:T(8,128)(2,1)S(1)} %get-tuple-element.22), channel_id=1, source_target_pairs={{0,2},{1,3},{2,0},{3,1},{4,6},{5,7},{6,4},{7,5},{8,10},{9,11},{10,... | collective-permute-start | bytes 221192 | tf_op jit(solution)/shard_map/ppermute | solution.py:430
  29.0 0.5 %collective-permute-start = (bf16[288,128]{1,0:T(8,128)(2,1)S(1)}, bf16[288,128]{1,0:T(8,128)(2,1)S(1)}, u32[]{:S(2)}, u32[]{:S(2)}) collective-permute-start(bf16[288,128]{1,0:T(8,128)(2,1)S(1)} %get-tuple-element.22), channel_id=1, source_target_pairs={{0,1},{1,0},{2,3},{3,2},{4,5},{5,4},{6,7},{7,6},{8,9},{9,8},{10,11... | collective-permute-start | bytes 221192 | tf_op jit(solution)/shard_map/ppermute | solution.py:430
  29.5 1.9 %collective-permute-done.2 = bf16[288,128]{1,0:T(8,128)(2,1)S(1)} collective-permute-done((bf16[288,128]{1,0:T(8,128)(2,1)S(1)}, bf16[288,128]{1,0:T(8,128)(2,1)S(1)}, u32[]{:S(2)}, u32[]{:S(2)}) %collective-permute-start.2) | collective-permute-done | bytes 73760 | tf_op jit(solution)/shard_map/ppermute | solution.py:430
  31.4 1.4 %collective-permute-done.1 = bf16[288,128]{1,0:T(8,128)(2,1)S(1)} collective-permute-done((bf16[288,128]{1,0:T(8,128)(2,1)S(1)}, bf16[288,128]{1,0:T(8,128)(2,1)S(1)}, u32[]{:S(2)}, u32[]{:S(2)}) %collective-permute-start.1) | collective-permute-done | bytes 73760 | tf_op jit(solution)/shard_map/ppermute | solution.py:430
  32.8 0.5 %collective-permute-done = bf16[288,128]{1,0:T(8,128)(2,1)S(1)} collective-permute-done((bf16[288,128]{1,0:T(8,128)(2,1)S(1)}, bf16[288,128]{1,0:T(8,128)(2,1)S(1)}, u32[]{:S(2)}, u32[]{:S(2)}) %collective-permute-start) | collective-permute-done | bytes 73760 | tf_op jit(solution)/shard_map/ppermute | solution.py:430
  33.4 0.7 %fusion.2.product_ref = f32[16,128]{1,0:T(8,128)S(1)} fusion(bf16[128,72,128]{2,1,0:T(8,128)(2,1)S(1)} %get-tuple-element.23, bf16[16,72,128]{2,1,0:T(8,128)(2,1)S(1)} %bitcast.11), kind=kOutput, calls=%fused_computation.2 | convolution fusion | flops 37748736 | bytes 2662400 | tf_op jit(solution)/shard_map/dot_general | solution.py:433
  34.1 0.1 share.1
  34.2 8.3 %all_to_all.17.copies_ref = f32[8,16,128]{2,1,0:T(8,128)S(1)} all-to-all(f32[8,16,128]{2,1,0:T(8,128)S(1)} %share.1), channel_id=1, replica_groups=mesh['pw'=8,'band'=4] {'pw'}, dimensions={0} | all-to-all | bytes 131072 | tf_op jit(solution)/shard_map/all_to_all | solution.py:442
  42.5 0.8 %finish.1 = (f32[144,128]{1,0:T(8,128)}, f32[2,4,64]{2,1,0:T(4,128)}, f32[2,4,64]{2,1,0:T(4,128)}) custom-call(s32[1]{0:T(128)} %bitcast.5.band_ref, f32[8,16,128]{2,1,0:T(8,128)S(1)} %all_to_all.17.copies_ref, f32[144,128]{1,0:T(8,128)S(1)} %get-tuple-element.27.image_ref, f32[144,128]{1,0:T(8,128)S(1)} %get-tuple-element.20.vector_ref), custom_call_target="tpu_custom_call" | custom-call | tf_op jit(solution)/shard_map/finish/pallas_call | solution.py:401
  (1 shorter events, 0.0 us)
Async XLA Ops:
  0.6 25.1 %copy-start = (bf16[288,256]{1,0:T(8,128)(2,1)S(1)}, bf16[288,256]{1,0:T(8,128)(2,1)}, u32[]{:S(2)}) copy-start(bf16[288,256]{1,0:T(8,128)(2,1)} %constant.22.clone.table_ref) | copy-start | bytes 442372
  26.0 5.4 %collective-permute-start.2 = (bf16[288,128]{1,0:T(8,128)(2,1)S(1)}, bf16[288,128]{1,0:T(8,128)(2,1)S(1)}, u32[]{:S(2)}, u32[]{:S(2)}) collective-permute-start(bf16[288,128]{1,0:T(8,128)(2,1)S(1)} %get-tuple-element.22), channel_id=1, source_target_pairs={{0,3},{1,2},{2,1},{3,0},{4,7},{5,6},{6,5},{7,4},{8,11},{9,10},{10,... | collective-permute-start | bytes 221192 | tf_op jit(solution)/shard_map/ppermute | solution.py:430
  28.5 4.4 %collective-permute-start.1 = (bf16[288,128]{1,0:T(8,128)(2,1)S(1)}, bf16[288,128]{1,0:T(8,128)(2,1)S(1)}, u32[]{:S(2)}, u32[]{:S(2)}) collective-permute-start(bf16[288,128]{1,0:T(8,128)(2,1)S(1)} %get-tuple-element.22), channel_id=1, source_target_pairs={{0,2},{1,3},{2,0},{3,1},{4,6},{5,7},{6,4},{7,5},{8,10},{9,11},{10,... | collective-permute-start | bytes 221192 | tf_op jit(solution)/shard_map/ppermute | solution.py:430
  29.0 4.4 %collective-permute-start = (bf16[288,128]{1,0:T(8,128)(2,1)S(1)}, bf16[288,128]{1,0:T(8,128)(2,1)S(1)}, u32[]{:S(2)}, u32[]{:S(2)}) collective-permute-start(bf16[288,128]{1,0:T(8,128)(2,1)S(1)} %get-tuple-element.22), channel_id=1, source_target_pairs={{0,1},{1,0},{2,3},{3,2},{4,5},{5,4},{6,7},{7,6},{8,9},{9,8},{10,11... | collective-permute-start | bytes 221192 | tf_op jit(solution)/shard_map/ppermute | solution.py:430

commit v8 on v7

--- a/solution.py
+++ b/solution.py
@@ -268,7 +268,7 @@
                 low.append((lines - high[-1].astype(f32)).astype(bf16))
             high, low = jnp.concatenate(high, 1), jnp.concatenate(low, 1)
             field_ref[first // 2] = jnp.dot(xb_ref[...], jnp.concatenate([high, high, low], 0), preferred_element_type=f32)
-        for copy in (pot_copy, tables[1], tables[2]):
+        for copy in (pot_copy, tables[1]):
             copy.wait()
         for first in range(0, rows, 2):
             weight = jnp.concatenate([pot_ref[first], pot_ref[first + 1]], 1)
@@ -281,6 +281,7 @@
                         part * box : (part + 1) * box, index * grid : (index + 1) * grid
                     ]
 
+        tables[2].wait()
         lines = jnp.concatenate([b_ref[0], b_ref[1]], 1).astype(bf16)
         boxed = jnp.dot(lines, yf_ref[...], preferred_element_type=f32)
         boxed = boxed[:, : 2 * line] + boxed[:, 2 * line :]

time: 43.5 us -> 43.5 us (level)
  no operation moved by 1% of the time
where the time goes in v8:
time: 43.5 us; the launch traced here: 43.3 us
  blocking collectives  28.8 us (66%)
  Pallas kernels  5.66 us (13%)
  waiting for transfers between devices  3.81 us (9%)
  starting transfers between devices  3.55 us (8%)
  matrix products  0.7 us (2%)
  between operations  0.67 us (2%)
    all_to_all x1, blocking collectives, shards(): lax.all_to_all(moving, 'pw', split_axis=0, concat_axis=0, tiled=True)  12.2 us
    all_to_all x1, blocking collectives, shards(): lax.all_to_all(copies, 'pw', split_axis=0, concat_axis=0, tiled=True)  8.31 us
    all_to_all x1, blocking collectives, shards(): lax.all_to_all(picked, 'pw', split_axis=0, concat_axis=0, tiled=True)  8.3 us
    pallas_call x4, Pallas kernels, call_on_chip(): pl.pallas_call(kernel, out_shape=tuple((pltpu.VMEM(shape, dtype) for shap...  4.89 us
    ppermute x3, waiting for transfers between devices, shards(): lax.ppermute(rounded, 'band', [(i, i ^ step) for i in range(band_total)])  3.81 us
    ppermute x3, starting transfers between devices, shards(): lax.ppermute(rounded, 'band', [(i, i ^ step) for i in range(band_total)])  3.55 us
  transfers between devices with their start and end apart: 3, of which 3 were waited for; matrix products, arithmetic and copies ran while one was open for 0% of the time, Pallas kernels for 0%

profile of v8, /device:TPU:0, one launch (start us, length us, event | category | flops | bytes accessed | tf_op | source)
XLA Modules:
  0.0 43.3 jit_solution(4177093770042972889)
XLA Ops:
  0.6 0.0 copy-start
  0.6 1.3 %spread_sticks.1 = (bf16[8,40,128]{2,1,0:T(8,128)(2,1)S(1)}, f32[144,128]{1,0:T(8,128)S(1)}, s32[1,128]{1,0:T(1,128)S(1)}, bf16[256,256]{1,0:T(8,128)(2,1)S(1)}) custom-call(f32[144,128]{1,0:T(8,128)} %bitcast.12, bf16[256,432]{1,0:T(8,128)(2,1)} %constant.21.clone.refs_1_, s32[1,128]{1,0:T(1,128)} %bitcast.13, bf16[256,256]{1,0:T(8,128)(2,1)} %constant.8.clone.refs_3_), custom_call_target="tpu_custom_call" | custom-call | tf_op jit(solution)/shard_map/spread_sticks/pallas_call | solution.py:100
  1.9 12.2 %all_to_all.15.in_ref = bf16[8,40,128]{2,1,0:T(8,128)(2,1)S(1)} all-to-all(bf16[8,40,128]{2,1,0:T(8,128)(2,1)S(1)} %get-tuple-element.17), channel_id=1, replica_groups=mesh['pw'=8,'band'=4] {'pw'}, dimensions={0} | all-to-all | bytes 163840 | tf_op jit(solution)/shard_map/all_to_all | solution.py:424
  14.2 3.3 %apply_planes.1 = (bf16[8,32,128]{2,1,0:T(8,128)(2,1)S(1)}, bf16[128,72,128]{2,1,0:T(8,128)(2,1)S(1)}) custom-call(bf16[8,40,128]{2,1,0:T(8,128)(2,1)S(1)} %all_to_all.15.in_ref, bf16[256,256]{1,0:T(8,128)(2,1)S(1)} %get-tuple-element.18.yb_ref, bf16[256,240]{1,0:T(8,128)(2,1)} %constant.18.clone.refs_0_, f32[16,128,128]{2,1,0:T(8,128)} %refs_1_.2, ...), custom_call_target="tpu_custom_call" | custom-call | tf_op jit(solution)/shard_map/apply_planes/pallas_call | solution.py:100
  17.5 8.3 %all_to_all.16 = bf16[8,32,128]{2,1,0:T(8,128)(2,1)S(1)} all-to-all(bf16[8,32,128]{2,1,0:T(8,128)(2,1)S(1)} %get-tuple-element.19), channel_id=1, replica_groups=mesh['pw'=8,'band'=4] {'pw'}, dimensions={0} | all-to-all | bytes 131072 | tf_op jit(solution)/shard_map/all_to_all | solution.py:426
  25.8 0.0 copy-done
  25.8 0.2 image_sticks.1
  26.0 2.5 %collective-permute-start.2 = (bf16[288,128]{1,0:T(8,128)(2,1)S(1)}, bf16[288,128]{1,0:T(8,128)(2,1)S(1)}, u32[]{:S(2)}, u32[]{:S(2)}) collective-permute-start(bf16[288,128]{1,0:T(8,128)(2,1)S(1)} %get-tuple-element.22), channel_id=1, source_target_pairs={{0,3},{1,2},{2,1},{3,0},{4,7},{5,6},{6,5},{7,4},{8,11},{9,10},{10,... | collective-permute-start | bytes 221192 | tf_op jit(solution)/shard_map/ppermute | solution.py:431
  28.5 0.5 %collective-permute-start.1 = (bf16[288,128]{1,0:T(8,128)(2,1)S(1)}, bf16[288,128]{1,0:T(8,128)(2,1)S(1)}, u32[]{:S(2)}, u32[]{:S(2)}) collective-permute-start(bf16[288,128]{1,0:T(8,128)(2,1)S(1)} %get-tuple-element.22), channel_id=1, source_target_pairs={{0,2},{1,3},{2,0},{3,1},{4,6},{5,7},{6,4},{7,5},{8,10},{9,11},{10,... | collective-permute-start | bytes 221192 | tf_op jit(solution)/shard_map/ppermute | solution.py:431
  29.0 0.5 %collective-permute-start = (bf16[288,128]{1,0:T(8,128)(2,1)S(1)}, bf16[288,128]{1,0:T(8,128)(2,1)S(1)}, u32[]{:S(2)}, u32[]{:S(2)}) collective-permute-start(bf16[288,128]{1,0:T(8,128)(2,1)S(1)} %get-tuple-element.22), channel_id=1, source_target_pairs={{0,1},{1,0},{2,3},{3,2},{4,5},{5,4},{6,7},{7,6},{8,9},{9,8},{10,11... | collective-permute-start | bytes 221192 | tf_op jit(solution)/shard_map/ppermute | solution.py:431
  29.6 1.9 %collective-permute-done.2 = bf16[288,128]{1,0:T(8,128)(2,1)S(1)} collective-permute-done((bf16[288,128]{1,0:T(8,128)(2,1)S(1)}, bf16[288,128]{1,0:T(8,128)(2,1)S(1)}, u32[]{:S(2)}, u32[]{:S(2)}) %collective-permute-start.2) | collective-permute-done | bytes 73760 | tf_op jit(solution)/shard_map/ppermute | solution.py:431
  31.4 1.4 %collective-permute-done.1 = bf16[288,128]{1,0:T(8,128)(2,1)S(1)} collective-permute-done((bf16[288,128]{1,0:T(8,128)(2,1)S(1)}, bf16[288,128]{1,0:T(8,128)(2,1)S(1)}, u32[]{:S(2)}, u32[]{:S(2)}) %collective-permute-start.1) | collective-permute-done | bytes 73760 | tf_op jit(solution)/shard_map/ppermute | solution.py:431
  32.9 0.5 %collective-permute-done = bf16[288,128]{1,0:T(8,128)(2,1)S(1)} collective-permute-done((bf16[288,128]{1,0:T(8,128)(2,1)S(1)}, bf16[288,128]{1,0:T(8,128)(2,1)S(1)}, u32[]{:S(2)}, u32[]{:S(2)}) %collective-permute-start) | collective-permute-done | bytes 73760 | tf_op jit(solution)/shard_map/ppermute | solution.py:431
  33.4 0.7 %fusion.2.product_ref = f32[16,128]{1,0:T(8,128)S(1)} fusion(bf16[128,72,128]{2,1,0:T(8,128)(2,1)S(1)} %get-tuple-element.23, bf16[16,72,128]{2,1,0:T(8,128)(2,1)S(1)} %bitcast.11), kind=kOutput, calls=%fused_computation.2 | convolution fusion | flops 37748736 | bytes 2662400 | tf_op jit(solution)/shard_map/dot_general | solution.py:434
  34.1 0.1 share.1
  34.2 8.3 %all_to_all.17.copies_ref = f32[8,16,128]{2,1,0:T(8,128)S(1)} all-to-all(f32[8,16,128]{2,1,0:T(8,128)S(1)} %share.1), channel_id=1, replica_groups=mesh['pw'=8,'band'=4] {'pw'}, dimensions={0} | all-to-all | bytes 131072 | tf_op jit(solution)/shard_map/all_to_all | solution.py:443
  42.5 0.8 %finish.1 = (f32[144,128]{1,0:T(8,128)}, f32[2,4,64]{2,1,0:T(4,128)}, f32[2,4,64]{2,1,0:T(4,128)}) custom-call(s32[1]{0:T(128)} %bitcast.5.band_ref, f32[8,16,128]{2,1,0:T(8,128)S(1)} %all_to_all.17.copies_ref, f32[144,128]{1,0:T(8,128)S(1)} %get-tuple-element.27.image_ref, f32[144,128]{1,0:T(8,128)S(1)} %get-tuple-element.20.vector_ref), custom_call_target="tpu_custom_call" | custom-call | tf_op jit(solution)/shard_map/finish/pallas_call | solution.py:402
  (1 shorter events, 0.0 us)
Async XLA Ops:
  0.6 25.2 %copy-start = (bf16[288,256]{1,0:T(8,128)(2,1)S(1)}, bf16[288,256]{1,0:T(8,128)(2,1)}, u32[]{:S(2)}) copy-start(bf16[288,256]{1,0:T(8,128)(2,1)} %constant.22.clone.table_ref) | copy-start | bytes 442372
  26.0 5.4 %collective-permute-start.2 = (bf16[288,128]{1,0:T(8,128)(2,1)S(1)}, bf16[288,128]{1,0:T(8,128)(2,1)S(1)}, u32[]{:S(2)}, u32[]{:S(2)}) collective-permute-start(bf16[288,128]{1,0:T(8,128)(2,1)S(1)} %get-tuple-element.22), channel_id=1, source_target_pairs={{0,3},{1,2},{2,1},{3,0},{4,7},{5,6},{6,5},{7,4},{8,11},{9,10},{10,... | collective-permute-start | bytes 221192 | tf_op jit(solution)/shard_map/ppermute | solution.py:431
  28.5 4.4 %collective-permute-start.1 = (bf16[288,128]{1,0:T(8,128)(2,1)S(1)}, bf16[288,128]{1,0:T(8,128)(2,1)S(1)}, u32[]{:S(2)}, u32[]{:S(2)}) collective-permute-start(bf16[288,128]{1,0:T(8,128)(2,1)S(1)} %get-tuple-element.22), channel_id=1, source_target_pairs={{0,2},{1,3},{2,0},{3,1},{4,6},{5,7},{6,4},{7,5},{8,10},{9,11},{10,... | collective-permute-start | bytes 221192 | tf_op jit(solution)/shard_map/ppermute | solution.py:431
  29.0 4.4 %collective-permute-start = (bf16[288,128]{1,0:T(8,128)(2,1)S(1)}, bf16[288,128]{1,0:T(8,128)(2,1)S(1)}, u32[]{:S(2)}, u32[]{:S(2)}) collective-permute-start(bf16[288,128]{1,0:T(8,128)(2,1)S(1)} %get-tuple-element.22), channel_id=1, source_target_pairs={{0,1},{1,0},{2,3},{3,2},{4,5},{5,4},{6,7},{7,6},{8,9},{9,8},{10,11... | collective-permute-start | bytes 221192 | tf_op jit(solution)/shard_map/ppermute | solution.py:431
